TPU v7x, 128 devices: a whole 4x4x4 slice. The times are simulated.
128 devices in a mesh: fib: 8 (over y, core), len: 4 (over x), emg: 4 (over z).
Axes of the slice: x: 4, y: 4, z: 4, core: 2. Of those that a mesh axis runs over, the one named last changes fastest.
Arguments:
- states: float32 [57, 256, 4096], P(None, 'len', ('fib', 'emg')), may hold values from -6 to 6
- voltage: float32 [256, 4096], P('len', ('fib', 'emg')), may hold values from -6 to 6
- coupling: float32 [57, 57], replicated, may hold values from -0.75 to 0.75
- decay_rates: float32 [57], replicated, may hold values from 0.05 to 1.9
- volt_gain: float32 [57], replicated, may hold values from -4 to 4
- current_weights: float32 [57], replicated, may hold values from -0.75 to 0.75
- fibre_home: int32 [4096, 1], P(('fib', 'emg')), may hold values from 0 to 31; in each aligned block of 128 rows (0 to 127, 128 to 255, ...) at most 12 rows name the same one
- cross_cell: int32 [4096], P(('fib', 'emg')), may hold values from 0 to 1023
- motor_unit: int32 [4096], P(('fib', 'emg')), may hold values from 0 to 99
- stim_step: int32 [100], replicated, may hold values from 0 to 2
- tissue: float32 [128, 64, 512], P('len', 'fib', 'emg'), may hold values from 0.5 to 2
Outputs:
- states_out: float32 [57, 256, 4096], P(None, 'len', ('fib', 'emg'))
- voltage_out: float32 [256, 4096], P('len', ('fib', 'emg'))
- potential: float32 [2, 128, 64, 512], P(None, 'len', 'fib', 'emg')
Inputs may be any that keep to these rules, and one draw needn't show every extreme that they name: `fibre_home`: the fibres of one fib and emg index name any one brick column at most 12 times, and some brick column is named exactly 12 times by the fibres of some index. `stim_step`: A value of 2 means the motor unit does not fire in this window.
All inputs are finite; a program needn't handle non-finite values.
Results may differ from a plain program's by a relative error of at most 0.0003.
Values sent between devices are 32-bit elements; how exact they have to be, the bound alone decides.
A program may use at most 64 MiB of HBM per device.

v0:
```python
import jax
import jax.numpy as jnp
from jax import lax
from jax.sharding import PartitionSpec as P

STEPS = 2
SWEEPS = 4
NPC = 2


time_step = 0.5
conductance = 2000.0
amplitude = 200.0
band_half = 4
low_bound = 0.5
high_bound = 14.0


def with_halo(block, sides, width):
    for axis, dim in sides:
        count = lax.axis_size(axis)
        forward = [(i, i + 1) for i in range(count - 1)]
        backward = [(target, source) for source, target in forward]
        low = lax.ppermute(
            lax.slice_in_dim(block, block.shape[dim] - width, None, axis=dim), axis, forward
        )
        high = lax.ppermute(lax.slice_in_dim(block, 0, width, axis=dim), axis, backward)
        block = jnp.concatenate([low, block, high], axis=dim)
    return block


def neighbours(padded, values, tissue):
    beside = padded[2:, 1:-1, 1:-1] + padded[:-2, 1:-1, 1:-1]
    beside = beside + padded[1:-1, 2:, 1:-1] + padded[1:-1, :-2, 1:-1]
    beside = beside + padded[1:-1, 1:-1, 2:] + padded[1:-1, 1:-1, :-2]
    return (6.0 + tissue) * values - beside


def chebyshev(source, operate):
    middle = 0.5 * (high_bound + low_bound)
    spread = 0.5 * (high_bound - low_bound)
    ratio_value = middle / spread
    weight_now = 1.0 / ratio_value
    solution = jnp.zeros_like(source)
    residual = source
    direction = source / middle
    for sweep_index in range(SWEEPS):
        solution = solution + direction
        if sweep_index + 1 < SWEEPS:
            residual = residual - operate(direction)
            weight_next = 1.0 / (2.0 * ratio_value - weight_now)
            direction = weight_next * weight_now * direction + 2.0 * weight_next / spread * residual
            weight_now = weight_next
    return solution


def face_operator(values, tissue):
    padded = with_halo(values, (("fib", 1), ("len", 0), ("emg", 2)), 1)
    return neighbours(padded, values, tissue)


def reduced_solve(matrix, rhs_rows):
    order_size = matrix.shape[0]
    for pivot_index in range(order_size):
        for row_index in range(pivot_index + 1, order_size):
            factor = matrix[row_index, pivot_index] / matrix[pivot_index, pivot_index]
            matrix = matrix.at[row_index].add(-factor * matrix[pivot_index])
            rhs_rows = rhs_rows.at[row_index].add(-factor * rhs_rows[pivot_index])
    solved = [None] * order_size
    for pivot_index in reversed(range(order_size)):
        running = rhs_rows[pivot_index]
        for column_index in range(pivot_index + 1, order_size):
            running = running - matrix[pivot_index, column_index] * solved[column_index]
        solved[pivot_index] = running / matrix[pivot_index, pivot_index]
    return jnp.stack(solved)


def cable_solve(right_side, diagonals, spikes):
    sub_diag, main_diag, super_diag = diagonals
    local_y = lax.linalg.tridiagonal_solve(sub_diag, main_diag, super_diag, right_side)
    first_spike = spikes[:, 0]
    last_spike = spikes[:, 1]
    end_values = jnp.concatenate([local_y[:1], local_y[-1:]], axis=0)
    coeffs = jnp.stack([first_spike[0], first_spike[-1], last_spike[0], last_spike[-1]])
    all_ends, all_coeffs = (
        lax.all_gather(end_values, "len", axis=0, tiled=True),
        lax.all_gather(coeffs, "len", axis=0, tiled=True),
    )
    shards = lax.axis_size("len")
    matrix = jnp.eye(2 * shards, dtype=jnp.float32)
    for shard_index in range(shards):
        if shard_index > 0:
            matrix = matrix.at[2 * shard_index, 2 * shard_index - 1].set(
                -conductance * all_coeffs[4 * shard_index]
            )
            matrix = matrix.at[2 * shard_index + 1, 2 * shard_index - 1].set(
                -conductance * all_coeffs[4 * shard_index + 1]
            )
        if shard_index + 1 < shards:
            matrix = matrix.at[2 * shard_index, 2 * shard_index + 2].set(
                -conductance * all_coeffs[4 * shard_index + 2]
            )
            matrix = matrix.at[2 * shard_index + 1, 2 * shard_index + 2].set(
                -conductance * all_coeffs[4 * shard_index + 3]
            )
    interface = reduced_solve(matrix, all_ends)
    blank_row = jnp.zeros((1, interface.shape[1]), jnp.float32)
    padded_ends = jnp.concatenate([blank_row, interface, blank_row], axis=0)
    my_shard = lax.axis_index("len")
    left_value = lax.dynamic_slice_in_dim(padded_ends, 2 * my_shard, 1, 0)
    right_value = lax.dynamic_slice_in_dim(padded_ends, 2 * my_shard + 3, 1, 0)
    return (
        local_y
        + conductance * left_value * first_spike[:, None]
        + conductance * right_value * last_spike[:, None]
    )


def pack_rows(payload, fibre_home, cross_cell, groups):
    fibre_count = payload.shape[1]
    capacity = 3 * fibre_count // groups
    home_brick = fibre_home[:, 0]
    member = (home_brick[:, None] == jnp.arange(groups, dtype=jnp.int32)[None, :]).astype(jnp.int32)
    earlier = jnp.cumsum(member, axis=0) - member
    rank_value = jnp.sum(earlier * member, axis=1)
    slot_index = home_brick * capacity + rank_value
    select = slot_index[None, :] == jnp.arange(groups * capacity, dtype=jnp.int32)[:, None]
    rows_sent = jnp.einsum(
        "sf,nf->sn", select.astype(jnp.float32), payload, precision=lax.Precision.HIGHEST
    )
    cells_sent = jnp.sum(jnp.where(select, cross_cell[None, :] + 1, 0), axis=1) - 1
    return (
        rows_sent.reshape(groups, capacity, payload.shape[0]),
        cells_sent.reshape(groups, capacity),
    )


def on_device(
    states,
    voltage,
    coupling,
    decay_rates,
    volt_gain,
    current_weights,
    fibre_home,
    cross_cell,
    motor_unit,
    stim_step,
    tissue,
):
    length_nodes, fibre_count = voltage.shape
    bin_cells, brick_rows, brick_depth = tissue.shape
    cells_total = brick_rows * brick_depth
    groups = lax.axis_size("fib") * lax.axis_size("emg")
    my_shard = lax.axis_index("len")
    shards = lax.axis_size("len")
    node_index = jnp.arange(length_nodes, dtype=jnp.int32)
    at_start = my_shard == 0
    at_end = my_shard == shards - 1
    main_diag = jnp.full((length_nodes,), 1.0 + 2.0 * conductance, jnp.float32)
    main_diag = jnp.where((node_index == 0) & at_start, 1.0 + conductance, main_diag)
    main_diag = jnp.where((node_index == length_nodes - 1) & at_end, 1.0 + conductance, main_diag)
    sub_diag = jnp.where(node_index == 0, 0.0, -conductance).astype(jnp.float32)
    super_diag = jnp.where(node_index == length_nodes - 1, 0.0, -conductance).astype(jnp.float32)
    diagonals = (sub_diag, main_diag, super_diag)
    unit_columns = jnp.stack([node_index == 0, node_index == length_nodes - 1], axis=1).astype(
        jnp.float32
    )
    spikes = lax.linalg.tridiagonal_solve(sub_diag, main_diag, super_diag, unit_columns)
    total_nodes = length_nodes * shards
    global_node = my_shard * length_nodes + node_index
    band_mask = (
        (global_node >= total_nodes // 2 - band_half) & (global_node < total_nodes // 2 + band_half)
    ).astype(jnp.float32)
    unit_match = motor_unit[:, None] == jnp.arange(stim_step.shape[0], dtype=jnp.int32)[None, :]
    potentials = []
    for step_index in range(STEPS):
        drive_term = (
            jnp.einsum("ij,jnf->inf", coupling, states, precision=lax.Precision.HIGHEST)
            + volt_gain[:, None, None] * voltage[None]
        )
        states = states + time_step * (jnp.tanh(drive_term) - decay_rates[:, None, None] * states)
        current = jnp.einsum("i,inf->nf", current_weights, states, precision=lax.Precision.HIGHEST)
        rows_sent, cells_sent = pack_rows(current, fibre_home, cross_cell, groups)
        got_rows, got_cells = (
            lax.all_to_all(rows_sent, ("fib", "emg"), split_axis=0, concat_axis=0, tiled=True),
            lax.all_to_all(cells_sent, ("fib", "emg"), split_axis=0, concat_axis=0, tiled=True),
        )
        rows_flat = got_rows.reshape(-1, got_rows.shape[2])
        binned = rows_flat.reshape(rows_flat.shape[0], bin_cells, NPC).sum(axis=2)
        cells_flat = got_cells.reshape(-1)
        cells_flat = jnp.where(cells_flat < 0, cells_total, cells_flat)
        source = (
            jnp.zeros((bin_cells, cells_total), jnp.float32)
            .at[:, cells_flat]
            .add(binned.T, mode="drop")
        )
        source = source.reshape(bin_cells, brick_rows, brick_depth)
        potentials.append(chebyshev(source, lambda values: face_operator(values, tissue)))
        active = jnp.any(unit_match & (stim_step[None, :] == step_index), axis=1).astype(
            jnp.float32
        )
        right_side = voltage + time_step * (
            amplitude * band_mask[:, None] * active[None, :] - current
        )
        voltage = cable_solve(right_side, diagonals, spikes)
    return (states, voltage, jnp.stack(potentials))


def solution(mesh):
    return jax.shard_map(
        on_device,
        mesh=mesh,
        in_specs=(
            P(None, "len", ("fib", "emg")),
            P("len", ("fib", "emg")),
            P(),
            P(),
            P(),
            P(),
            P(("fib", "emg"), None),
            P(("fib", "emg")),
            P(("fib", "emg")),
            P(),
            P("len", "fib", "emg"),
        ),
        out_specs=(
            P(None, "len", ("fib", "emg")),
            P("len", ("fib", "emg")),
            P(None, "len", "fib", "emg"),
        ),
        check_vma=False,
    )
```

profile of v0, /device:TPU:1, one launch (start us, length us, event | category | flops | bytes accessed | tf_op | source)
XLA Modules:
  0.0 740.7 jit_solution(6085449308562404587)
XLA Ops:
  4.1 9.6 %all-to-all-start = ((s32[32,1,12]{2,1,0:T(1,128)}), s32[32,1,12]{2,1,0:T(1,128)S(1)}, u32[]{:S(2)}, u32[]{:S(2)}) async-start(s32[32,1,12]{2,1,0:T(1,128)} %bitcast.489), calls=%async_computation | async-start | bytes 32768 | tf_op jit(solution)/shard_map/all_to_all | solution.py:187
  102.5 26.5 %subtract_divide_fusion = (f32[1,2]{0,1:T(2,128)S(1)}, f32[1,2]{0,1:T(2,128)S(1)}, f32[1,2]{0,1:T(2,128)S(1)}, f32[1,2]{0,1:T(2,128)S(1)}, f32[1,2]{0,1:T(2,128)...) fusion(f32[64,2]{0,1:T(2,128)S(1)} %add_convert_fusion, ...), kind=kLoop, calls=%fused_computation.280 | loop fusion | flops 248 | bytes 1004 | tf_op jit(solution)/shard_map/eval_jaxpr/div | solution.py:169
  170.4 38.9 %fusion.233 = (f32[1,2]{1,0:T(1,128)S(1)}, f32[2]{0:T(128)S(1)}, f32[2]{0:T(128)S(1)}, f32[2]{0:T(128)S(1)}, f32[2]{0:T(128)S(1)}, /*index=5*/f32[2]{0:T(128)S(1...) fusion(f32[]{:T(128)S(6)} %div.20398, ...), kind=kLoop, calls=%fused_computation.1070 | loop fusion | flops 376 | bytes 1332 | tf_op jit(solution)/shard_map/while/body/broadcast_in_dim | solution.py:169
  210.3 13.2 %subtract_bitcast_fusion = (f32[1,2]{1,0:T(1,128)S(1)}, f32[2]{0:T(128)S(1)}) fusion(f32[2]{0:T(128)S(1)} %reduce.237, f32[2]{0:T(128)S(1)} %reduce.238, f32[2]{0:T(128)S(1)} %get-tuple-element.1888, f32[2]{0:T(128)S(1)} %get-tuple-element.1887, f32[2]{0:T(128)S(1)} %get-tuple-element.1886, f32[2]{0:T(128)S(1)} %get-tuple-element.1885, ...), kind=kLoop, calls=%fused_computation.868 | loop fusion | flops 306 | bytes 732 | tf_op jit(solution)/shard_map/broadcast_in_dim | solution.py:169
  228.2 8.4 %all-reduce = f32[16]{0:T(128)S(1)} all-reduce(f32[16]{0:T(128)S(1)} %maximum_dynamic-update-slice_fusion), channel_id=1, replica_groups=mesh['fib'=8,'len'=4,'emg'=4] {'len'}, use_global_device_ids=true, to_apply=%add | all-reduce | flops 16 | bytes 128
  298.5 4.1 multiply_add_fusion
  305.3 40.1 %fusion.223 = (f32[1,128]{1,0:T(1,128)S(1)}, f32[128]{0:T(128)S(1)}, f32[128]{0:T(128)S(1)}, f32[128]{0:T(128)S(1)}, f32[128]{0:T(128)S(1)}, /*index=5*/f32[128]...) fusion(f32[]{:T(128)S(6)} %div.20398, ...), kind=kLoop, calls=%fused_computation.1060 | loop fusion | flops 24576 | bytes 54784 | tf_op jit(solution)/shard_map/while/body/broadcast_in_dim | solution.py:80
  345.4 25.2 %subtract_divide_fusion.156 = (f32[1,128]{1,0:T(1,128)S(1)}, f32[1,128]{1,0:T(1,128)S(1)}, f32[1,128]{1,0:T(1,128)S(1)}, f32[1,128]{1,0:T(1,128)S(1)}, f32[1,128...) fusion(f32[64,128]{1,0:T(8,128)S(1)} %multiply_add_fusion.8, ...), kind=kLoop, calls=%fused_computation.995 | loop fusion | flops 15360 | bytes 41792 | tf_op jit(solution)/shard_map/eval_jaxpr/div | solution.py:80
  370.7 13.9 %fusion.221 = (f32[1,128]{1,0:T(1,128)S(1)}, f32[128]{0:T(128)S(1)}) fusion(f32[128]{0:T(128)S(1)} %get-tuple-element.2033, f32[128]{0:T(128)S(1)} %get-tuple-element.2032, f32[128]{0:T(128)S(1)} %get-tuple-element.2031, f32[128]{0:T(128)S(1)} %get-tuple-element.2030, f32[128]{0:T(128)S(1)} %get-tuple-element.2029, f32[128]{0:T(128)S(1)} %get-tuple-element.2028, ...), kind=kLoop, calls=%fused_computation.1055 | loop fusion | flops 19712 | bytes 24928 | tf_op jit(solution)/shard_map/concatenate | solution.py:80
  384.6 5.2 all-gather
  396.3 13.9 %multiply_subtract_fusion = (f32[1,2]{0,1:T(2,128)S(1)}, f32[1,2]{0,1:T(2,128)S(1)}, f32[1,2]{0,1:T(2,128)S(1)}, f32[1,2]{0,1:T(2,128)S(1)}, f32[1,2]{0,1:T(2,12...) fusion(f32[1,2]{0,1:T(2,128)S(1)} %get-tuple-element.1989, ...), kind=kLoop, calls=%fused_computation.238 | loop fusion | flops 380 | bytes 1264 | tf_op jit(solution)/shard_map/eval_jaxpr/sub | solution.py:169
  418.4 22.2 %subtract_divide_fusion.88 = (f32[1,128]{1,0:T(1,128)S(1)}, f32[1,128]{1,0:T(1,128)S(1)}, f32[1,128]{1,0:T(1,128)S(1)}, f32[1,128]{1,0:T(1,128)S(1)}, f32[1,128]...) fusion(f32[8,128]{1,0:T(8,128)S(1)} %scatter-add.330, f32[]{:T(128)} %bitcast.369, ...), kind=kLoop, calls=%fused_computation.807 | loop fusion | flops 9472 | bytes 8868 | tf_op jit(solution)/shard_map/div | solution.py:74
  440.7 13.9 %multiply_subtract_fusion.124 = (f32[1,128]{1,0:T(1,128)S(1)}, f32[1,128]{1,0:T(1,128)S(1)}, f32[1,128]{1,0:T(1,128)S(1)}, f32[1,128]{1,0:T(1,128)S(1)}, f32[1,1...) fusion(f32[1,128]{1,0:T(1,128)S(1)} %get-tuple-element.2034, ...), kind=kLoop, calls=%fused_computation.953 | loop fusion | flops 24320 | bytes 54184 | tf_op jit(solution)/shard_map/eval_jaxpr/sub | solution.py:80
  454.9 4.7 fusion.3
  461.0 40.1 %fusion.243 = (f32[1,128]{1,0:T(1,128)S(1)}, f32[128]{0:T(128)S(1)}, f32[128]{0:T(128)S(1)}, f32[128]{0:T(128)S(1)}, f32[128]{0:T(128)S(1)}, /*index=5*/f32[128]...) fusion(f32[]{:T(128)S(6)} %div.20398, ...), kind=kLoop, calls=%fused_computation.1080 | loop fusion | flops 24576 | bytes 54784 | tf_op jit(solution)/shard_map/while/body/broadcast_in_dim | solution.py:80
  501.1 25.2 %subtract_divide_fusion.48 = (f32[1,128]{1,0:T(1,128)S(1)}, f32[1,128]{1,0:T(1,128)S(1)}, f32[1,128]{1,0:T(1,128)S(1)}, f32[1,128]{1,0:T(1,128)S(1)}, f32[1,128]...) fusion(f32[64,128]{1,0:T(8,128)S(1)} %multiply_add_fusion.6, ...), kind=kLoop, calls=%fused_computation.745 | loop fusion | flops 15360 | bytes 41792 | tf_op jit(solution)/shard_map/eval_jaxpr/div | solution.py:80
  526.4 13.9 %fusion.222 = (f32[1,128]{1,0:T(1,128)S(1)}, f32[128]{0:T(128)S(1)}) fusion(f32[128]{0:T(128)S(1)} %get-tuple-element.1736, f32[128]{0:T(128)S(1)} %get-tuple-element.1735, f32[128]{0:T(128)S(1)} %get-tuple-element.1734, f32[128]{0:T(128)S(1)} %get-tuple-element.1733, f32[128]{0:T(128)S(1)} %get-tuple-element.1732, f32[128]{0:T(128)S(1)} %get-tuple-element.1731, ...), kind=kLoop, calls=%fused_computation.1056 | loop fusion | flops 19712 | bytes 24928 | tf_op jit(solution)/shard_map/broadcast_in_dim | solution.py:80
  540.3 7.0 all-gather.1
  548.9 22.2 %subtract_divide_fusion.41 = (f32[1,128]{1,0:T(1,128)S(1)}, f32[1,128]{1,0:T(1,128)S(1)}, f32[1,128]{1,0:T(1,128)S(1)}, f32[1,128]{1,0:T(1,128)S(1)}, f32[1,128]...) fusion(f32[8,128]{1,0:T(8,128)S(1)} %scatter-add.371, f32[]{:T(128)} %bitcast.369, ...), kind=kLoop, calls=%fused_computation.670 | loop fusion | flops 9472 | bytes 8868 | tf_op jit(solution)/shard_map/div | solution.py:74
  571.1 13.9 %multiply_subtract_fusion.42 = (f32[1,128]{1,0:T(1,128)S(1)}, f32[1,128]{1,0:T(1,128)S(1)}, f32[1,128]{1,0:T(1,128)S(1)}, f32[1,128]{1,0:T(1,128)S(1)}, f32[1,12...) fusion(f32[1,128]{1,0:T(1,128)S(1)} %get-tuple-element.1737, ...), kind=kLoop, calls=%fused_computation.703 | loop fusion | flops 24320 | bytes 54184 | tf_op jit(solution)/shard_map/eval_jaxpr/sub | solution.py:80
  589.8 13.1 %all-to-all-start.2 = ((f32[32,1,768]{2,1,0:T(1,128)}), f32[32,1,768]{2,1,0:T(1,128)S(1)}, u32[]{:S(2)}, u32[]{:S(2)}) async-start(f32[32,1,768]{2,1,0:T(1,128)} %reshape.8392), calls=%async_computation.2 | async-start | bytes 196608 | tf_op jit(solution)/shard_map/all_to_all | solution.py:186
  604.2 6.1 all-to-all-done.2
  610.3 4.3 all-to-all-start.1
  638.1 4.0 collective-permute-start.21
  643.5 4.0 collective-permute-start.3
  652.5 4.0 collective-permute-start.5
  674.8 4.0 collective-permute-start.27
  680.2 4.0 collective-permute-start.9
  689.0 4.0 collective-permute-start.11
  711.4 4.0 collective-permute-start.33
  716.7 4.0 collective-permute-start.15
  725.3 4.0 collective-permute-start.17
  (453 shorter events, 151.5 us)
Async XLA Ops:
  4.1 585.7 %all-to-all-start = ((s32[32,1,12]{2,1,0:T(1,128)}), s32[32,1,12]{2,1,0:T(1,128)S(1)}, u32[]{:S(2)}, u32[]{:S(2)}) async-start(s32[32,1,12]{2,1,0:T(1,128)} %bitcast.489), calls=%async_computation | async-start | bytes 32768 | tf_op jit(solution)/shard_map/all_to_all | solution.py:187
  589.8 20.5 %all-to-all-start.2 = ((f32[32,1,768]{2,1,0:T(1,128)}), f32[32,1,768]{2,1,0:T(1,128)S(1)}, u32[]{:S(2)}, u32[]{:S(2)}) async-start(f32[32,1,768]{2,1,0:T(1,128)} %reshape.8392), calls=%async_computation.2 | async-start | bytes 196608 | tf_op jit(solution)/shard_map/all_to_all | solution.py:186
  610.3 15.7 %all-to-all-start.1 = ((f32[32,1,768]{2,1,0:T(1,128)}), f32[32,1,768]{2,1,0:T(1,128)S(1)}, u32[]{:S(2)}, u32[]{:S(2)}) async-start(f32[32,1,768]{2,1,0:T(1,128)} %reshape.8394), calls=%async_computation.1 | async-start | bytes 196608 | tf_op jit(solution)/shard_map/all_to_all | solution.py:186
  620.4 16.4 %collective-permute-start.19 = (f32[32,1,128]{2,1,0:T(1,128)S(1)}, f32[32,1,128]{2,1,0:T(1,128)S(1)}, u32[]{:S(2)}, u32[]{:S(2)}) collective-permute-start(f32[32,1,128]{2,1,0:T(1,128)S(1)} %get-tuple-element.2172), channel_id=1, source_target_pairs={{16,0},{32,16},{48,32},{64,48},{80,64},{96,80},{112,96},{17,1},{33... | collective-permute-start | bytes 49160 | tf_op jit(solution)/shard_map/ppermute | solution.py:27
  622.5 14.3 %collective-permute-start.18 = (f32[32,1,128]{2,1,0:T(1,128)S(1)}, f32[32,1,128]{2,1,0:T(1,128)S(1)}, u32[]{:S(2)}, u32[]{:S(2)}) collective-permute-start(f32[32,1,128]{2,1,0:T(1,128)S(1)} %get-tuple-element.2171), channel_id=1, source_target_pairs={{0,16},{16,32},{32,48},{48,64},{64,80},{80,96},{96,112},{1,17},{17... | collective-permute-start | bytes 49160 | tf_op jit(solution)/shard_map/ppermute | solution.py:24
  631.2 10.9 %collective-permute-start.1 = (f32[32,1,128]{2,1,0:T(1,128)S(1)}, f32[32,1,128]{2,1,0:T(1,128)S(1)}, u32[]{:S(2)}, u32[]{:S(2)}) collective-permute-start(f32[32,1,128]{2,1,0:T(1,128)S(1)} %get-tuple-element.2166), channel_id=1, source_target_pairs={{16,0},{32,16},{48,32},{64,48},{80,64},{96,80},{112,96},{17,1},{33... | collective-permute-start | bytes 49160 | tf_op jit(solution)/shard_map/ppermute | solution.py:27
  633.1 9.0 %collective-permute-start = (f32[32,1,128]{2,1,0:T(1,128)S(1)}, f32[32,1,128]{2,1,0:T(1,128)S(1)}, u32[]{:S(2)}, u32[]{:S(2)}) collective-permute-start(f32[32,1,128]{2,1,0:T(1,128)S(1)} %get-tuple-element.2165), channel_id=1, source_target_pairs={{0,16},{16,32},{32,48},{48,64},{64,80},{80,96},{96,112},{1,17},{17... | collective-permute-start | bytes 49160 | tf_op jit(solution)/shard_map/ppermute | solution.py:24
  636.8 10.6 %collective-permute-start.20 = (f32[1,10,128]{2,1,0:T(8,128)S(1)}, f32[1,10,128]{2,1,0:T(8,128)S(1)}, u32[]{:S(2)}, u32[]{:S(2)}) collective-permute-start(f32[1,10,128]{2,1,0:T(8,128)S(1)} %get-tuple-element.2160), channel_id=1, source_target_pairs={{4,0},{8,4},{12,8},{5,1},{9,5},{13,9},{6,2},{10,6},{14,10},{7,3},{... | collective-permute-start | bytes 15368 | tf_op jit(solution)/shard_map/ppermute | solution.py:27
  638.1 9.3 %collective-permute-start.21 = (f32[1,10,128]{2,1,0:T(8,128)S(1)}, f32[1,10,128]{2,1,0:T(8,128)S(1)}, u32[]{:S(2)}, u32[]{:S(2)}) collective-permute-start(f32[1,10,128]{2,1,0:T(8,128)S(1)} %get-tuple-element.2159), channel_id=1, source_target_pairs={{0,4},{4,8},{8,12},{1,5},{5,9},{9,13},{2,6},{6,10},{10,14},{3,7},{... | collective-permute-start | bytes 15368 | tf_op jit(solution)/shard_map/ppermute | solution.py:24
  642.2 10.1 %collective-permute-start.2 = (f32[1,10,128]{2,1,0:T(8,128)S(1)}, f32[1,10,128]{2,1,0:T(8,128)S(1)}, u32[]{:S(2)}, u32[]{:S(2)}) collective-permute-start(f32[1,10,128]{2,1,0:T(8,128)S(1)} %get-tuple-element.2154), channel_id=1, source_target_pairs={{4,0},{8,4},{12,8},{5,1},{9,5},{13,9},{6,2},{10,6},{14,10},{7,3},{... | collective-permute-start | bytes 15368 | tf_op jit(solution)/shard_map/ppermute | solution.py:27
  647.7 10.1 %collective-permute-start.23 = (f32[34,10,1]{2,1,0:T(8,128)S(1)}, f32[34,10,1]{2,1,0:T(8,128)S(1)}, u32[]{:S(2)}, u32[]{:S(2)}) collective-permute-start(f32[34,10,1]{2,1,0:T(8,128)S(1)} %get-tuple-element.2148), channel_id=1, source_target_pairs={{0,1},{1,2},{2,3},{4,5},{5,6},{6,7},{8,9},{9,10},{10,11},{12,13},{... | collective-permute-start | bytes 4088 | tf_op jit(solution)/shard_map/ppermute | solution.py:24
  650.9 9.9 %collective-permute-start.22 = (f32[34,10,1]{2,1,0:T(8,128)S(1)}, f32[34,10,1]{2,1,0:T(8,128)S(1)}, u32[]{:S(2)}, u32[]{:S(2)}) collective-permute-start(f32[34,10,1]{2,1,0:T(8,128)S(1)} %get-tuple-element.2147), channel_id=1, source_target_pairs={{1,0},{2,1},{3,2},{5,4},{6,5},{7,6},{9,8},{10,9},{11,10},{13,12},{... | collective-permute-start | bytes 4088 | tf_op jit(solution)/shard_map/ppermute | solution.py:27
  652.5 15.1 %collective-permute-start.5 = (f32[34,10,1]{2,1,0:T(8,128)S(1)}, f32[34,10,1]{2,1,0:T(8,128)S(1)}, u32[]{:S(2)}, u32[]{:S(2)}) collective-permute-start(f32[34,10,1]{2,1,0:T(8,128)S(1)} %get-tuple-element.2142), channel_id=1, source_target_pairs={{0,1},{1,2},{2,3},{4,5},{5,6},{6,7},{8,9},{9,10},{10,11},{12,13},{... | collective-permute-start | bytes 4088 | tf_op jit(solution)/shard_map/ppermute | solution.py:24
  656.5 11.1 %collective-permute-start.4 = (f32[34,10,1]{2,1,0:T(8,128)S(1)}, f32[34,10,1]{2,1,0:T(8,128)S(1)}, u32[]{:S(2)}, u32[]{:S(2)}) collective-permute-start(f32[34,10,1]{2,1,0:T(8,128)S(1)} %get-tuple-element.2141), channel_id=1, source_target_pairs={{1,0},{2,1},{3,2},{5,4},{6,5},{7,6},{9,8},{10,9},{11,10},{13,12},{... | collective-permute-start | bytes 4088 | tf_op jit(solution)/shard_map/ppermute | solution.py:27
  661.2 12.3 %collective-permute-start.25 = (f32[32,1,128]{2,1,0:T(1,128)S(1)}, f32[32,1,128]{2,1,0:T(1,128)S(1)}, u32[]{:S(2)}, u32[]{:S(2)}) collective-permute-start(f32[32,1,128]{2,1,0:T(1,128)S(1)} %get-tuple-element.2170), channel_id=1, source_target_pairs={{16,0},{32,16},{48,32},{64,48},{80,64},{96,80},{112,96},{17,1},{33... | collective-permute-start | bytes 49160 | tf_op jit(solution)/shard_map/ppermute | solution.py:27
  667.9 10.9 %collective-permute-start.7 = (f32[32,1,128]{2,1,0:T(1,128)S(1)}, f32[32,1,128]{2,1,0:T(1,128)S(1)}, u32[]{:S(2)}, u32[]{:S(2)}) collective-permute-start(f32[32,1,128]{2,1,0:T(1,128)S(1)} %get-tuple-element.2164), channel_id=1, source_target_pairs={{16,0},{32,16},{48,32},{64,48},{80,64},{96,80},{112,96},{17,1},{33... | collective-permute-start | bytes 49160 | tf_op jit(solution)/shard_map/ppermute | solution.py:27
  673.5 10.6 %collective-permute-start.26 = (f32[1,10,128]{2,1,0:T(8,128)S(1)}, f32[1,10,128]{2,1,0:T(8,128)S(1)}, u32[]{:S(2)}, u32[]{:S(2)}) collective-permute-start(f32[1,10,128]{2,1,0:T(8,128)S(1)} %get-tuple-element.2158), channel_id=1, source_target_pairs={{4,0},{8,4},{12,8},{5,1},{9,5},{13,9},{6,2},{10,6},{14,10},{7,3},{... | collective-permute-start | bytes 15368 | tf_op jit(solution)/shard_map/ppermute | solution.py:27
  674.8 9.3 %collective-permute-start.27 = (f32[1,10,128]{2,1,0:T(8,128)S(1)}, f32[1,10,128]{2,1,0:T(8,128)S(1)}, u32[]{:S(2)}, u32[]{:S(2)}) collective-permute-start(f32[1,10,128]{2,1,0:T(8,128)S(1)} %get-tuple-element.2157), channel_id=1, source_target_pairs={{0,4},{4,8},{8,12},{1,5},{5,9},{9,13},{2,6},{6,10},{10,14},{3,7},{... | collective-permute-start | bytes 15368 | tf_op jit(solution)/shard_map/ppermute | solution.py:24
  678.9 9.9 %collective-permute-start.8 = (f32[1,10,128]{2,1,0:T(8,128)S(1)}, f32[1,10,128]{2,1,0:T(8,128)S(1)}, u32[]{:S(2)}, u32[]{:S(2)}) collective-permute-start(f32[1,10,128]{2,1,0:T(8,128)S(1)} %get-tuple-element.2152), channel_id=1, source_target_pairs={{4,0},{8,4},{12,8},{5,1},{9,5},{13,9},{6,2},{10,6},{14,10},{7,3},{... | collective-permute-start | bytes 15368 | tf_op jit(solution)/shard_map/ppermute | solution.py:27
  684.4 10.0 %collective-permute-start.29 = (f32[34,10,1]{2,1,0:T(8,128)S(1)}, f32[34,10,1]{2,1,0:T(8,128)S(1)}, u32[]{:S(2)}, u32[]{:S(2)}) collective-permute-start(f32[34,10,1]{2,1,0:T(8,128)S(1)} %get-tuple-element.2146), channel_id=1, source_target_pairs={{0,1},{1,2},{2,3},{4,5},{5,6},{6,7},{8,9},{9,10},{10,11},{12,13},{... | collective-permute-start | bytes 4088 | tf_op jit(solution)/shard_map/ppermute | solution.py:24
  687.5 9.7 %collective-permute-start.28 = (f32[34,10,1]{2,1,0:T(8,128)S(1)}, f32[34,10,1]{2,1,0:T(8,128)S(1)}, u32[]{:S(2)}, u32[]{:S(2)}) collective-permute-start(f32[34,10,1]{2,1,0:T(8,128)S(1)} %get-tuple-element.2145), channel_id=1, source_target_pairs={{1,0},{2,1},{3,2},{5,4},{6,5},{7,6},{9,8},{10,9},{11,10},{13,12},{... | collective-permute-start | bytes 4088 | tf_op jit(solution)/shard_map/ppermute | solution.py:27
  689.0 15.1 %collective-permute-start.11 = (f32[34,10,1]{2,1,0:T(8,128)S(1)}, f32[34,10,1]{2,1,0:T(8,128)S(1)}, u32[]{:S(2)}, u32[]{:S(2)}) collective-permute-start(f32[34,10,1]{2,1,0:T(8,128)S(1)} %get-tuple-element.2140), channel_id=1, source_target_pairs={{0,1},{1,2},{2,3},{4,5},{5,6},{6,7},{8,9},{9,10},{10,11},{12,13},{... | collective-permute-start | bytes 4088 | tf_op jit(solution)/shard_map/ppermute | solution.py:24
  693.0 11.1 %collective-permute-start.10 = (f32[34,10,1]{2,1,0:T(8,128)S(1)}, f32[34,10,1]{2,1,0:T(8,128)S(1)}, u32[]{:S(2)}, u32[]{:S(2)}) collective-permute-start(f32[34,10,1]{2,1,0:T(8,128)S(1)} %get-tuple-element.2139), channel_id=1, source_target_pairs={{1,0},{2,1},{3,2},{5,4},{6,5},{7,6},{9,8},{10,9},{11,10},{13,12},{... | collective-permute-start | bytes 4088 | tf_op jit(solution)/shard_map/ppermute | solution.py:27
  697.5 12.6 %collective-permute-start.31 = (f32[32,1,128]{2,1,0:T(1,128)S(1)}, f32[32,1,128]{2,1,0:T(1,128)S(1)}, u32[]{:S(2)}, u32[]{:S(2)}) collective-permute-start(f32[32,1,128]{2,1,0:T(1,128)S(1)} %get-tuple-element.2168), channel_id=1, source_target_pairs={{16,0},{32,16},{48,32},{64,48},{80,64},{96,80},{112,96},{17,1},{33... | collective-permute-start | bytes 49160 | tf_op jit(solution)/shard_map/ppermute | solution.py:27
  704.5 10.9 %collective-permute-start.13 = (f32[32,1,128]{2,1,0:T(1,128)S(1)}, f32[32,1,128]{2,1,0:T(1,128)S(1)}, u32[]{:S(2)}, u32[]{:S(2)}) collective-permute-start(f32[32,1,128]{2,1,0:T(1,128)S(1)} %get-tuple-element.2162), channel_id=1, source_target_pairs={{16,0},{32,16},{48,32},{64,48},{80,64},{96,80},{112,96},{17,1},{33... | collective-permute-start | bytes 49160 | tf_op jit(solution)/shard_map/ppermute | solution.py:27
  710.1 10.6 %collective-permute-start.32 = (f32[1,10,128]{2,1,0:T(8,128)S(1)}, f32[1,10,128]{2,1,0:T(8,128)S(1)}, u32[]{:S(2)}, u32[]{:S(2)}) collective-permute-start(f32[1,10,128]{2,1,0:T(8,128)S(1)} %get-tuple-element.2156), channel_id=1, source_target_pairs={{4,0},{8,4},{12,8},{5,1},{9,5},{13,9},{6,2},{10,6},{14,10},{7,3},{... | collective-permute-start | bytes 15368 | tf_op jit(solution)/shard_map/ppermute | solution.py:27
  711.4 9.3 %collective-permute-start.33 = (f32[1,10,128]{2,1,0:T(8,128)S(1)}, f32[1,10,128]{2,1,0:T(8,128)S(1)}, u32[]{:S(2)}, u32[]{:S(2)}) collective-permute-start(f32[1,10,128]{2,1,0:T(8,128)S(1)} %get-tuple-element.2155), channel_id=1, source_target_pairs={{0,4},{4,8},{8,12},{1,5},{5,9},{9,13},{2,6},{6,10},{10,14},{3,7},{... | collective-permute-start | bytes 15368 | tf_op jit(solution)/shard_map/ppermute | solution.py:24
  715.4 9.6 %collective-permute-start.14 = (f32[1,10,128]{2,1,0:T(8,128)S(1)}, f32[1,10,128]{2,1,0:T(8,128)S(1)}, u32[]{:S(2)}, u32[]{:S(2)}) collective-permute-start(f32[1,10,128]{2,1,0:T(8,128)S(1)} %get-tuple-element.2150), channel_id=1, source_target_pairs={{4,0},{8,4},{12,8},{5,1},{9,5},{13,9},{6,2},{10,6},{14,10},{7,3},{... | collective-permute-start | bytes 15368 | tf_op jit(solution)/shard_map/ppermute | solution.py:27
  720.9 9.6 %collective-permute-start.35 = (f32[34,10,1]{2,1,0:T(8,128)S(1)}, f32[34,10,1]{2,1,0:T(8,128)S(1)}, u32[]{:S(2)}, u32[]{:S(2)}) collective-permute-start(f32[34,10,1]{2,1,0:T(8,128)S(1)} %get-tuple-element.2144), channel_id=1, source_target_pairs={{0,1},{1,2},{2,3},{4,5},{5,6},{6,7},{8,9},{9,10},{10,11},{12,13},{... | collective-permute-start | bytes 4088 | tf_op jit(solution)/shard_map/ppermute | solution.py:24
  723.8 9.7 %collective-permute-start.34 = (f32[34,10,1]{2,1,0:T(8,128)S(1)}, f32[34,10,1]{2,1,0:T(8,128)S(1)}, u32[]{:S(2)}, u32[]{:S(2)}) collective-permute-start(f32[34,10,1]{2,1,0:T(8,128)S(1)} %get-tuple-element.2143), channel_id=1, source_target_pairs={{1,0},{2,1},{3,2},{5,4},{6,5},{7,6},{9,8},{10,9},{11,10},{13,12},{... | collective-permute-start | bytes 4088 | tf_op jit(solution)/shard_map/ppermute | solution.py:27
  725.3 10.2 %collective-permute-start.17 = (f32[34,10,1]{2,1,0:T(8,128)S(1)}, f32[34,10,1]{2,1,0:T(8,128)S(1)}, u32[]{:S(2)}, u32[]{:S(2)}) collective-permute-start(f32[34,10,1]{2,1,0:T(8,128)S(1)} %get-tuple-element.2138), channel_id=1, source_target_pairs={{0,1},{1,2},{2,3},{4,5},{5,6},{6,7},{8,9},{9,10},{10,11},{12,13},{... | collective-permute-start | bytes 4088 | tf_op jit(solution)/shard_map/ppermute | solution.py:24
  729.3 10.0 %collective-permute-start.16 = (f32[34,10,1]{2,1,0:T(8,128)S(1)}, f32[34,10,1]{2,1,0:T(8,128)S(1)}, u32[]{:S(2)}, u32[]{:S(2)}) collective-permute-start(f32[34,10,1]{2,1,0:T(8,128)S(1)} %get-tuple-element.2137), channel_id=1, source_target_pairs={{1,0},{2,1},{3,2},{5,4},{6,5},{7,6},{9,8},{10,9},{11,10},{13,12},{... | collective-permute-start | bytes 4088 | tf_op jit(solution)/shard_map/ppermute | solution.py:27
  (18 other events, 2405.5 us)
where the time goes:
time: 756 us; the launch traced here: 741 us
  other arithmetic  341 us (45%)
  between operations  168 us (22%)
  starting transfers between devices  123 us (16%)
  local copies, waits for them, and re-layouts  56 us (7%)
  blocking collectives  20.7 us (3%)
  waiting for transfers between devices  20.6 us (3%)
  matrix products  12 us (2%)
    broadcast_in_dim x21, other arithmetic, cable_solve(): lax.linalg.tridiagonal_solve(sub_diag, main_diag, super_diag, right_side)  94.2 us
    ppermute x18, starting transfers between devices, with_halo(): lax.ppermute(lax.slice_in_dim(block, block.shape[dim] - width, None, axis...  65.1 us
    broadcast_in_dim x11, other arithmetic, on_device(): lax.linalg.tridiagonal_solve(sub_diag, main_diag, super_diag, unit_columns)  52.2 us
    div x2, other arithmetic, cable_solve(): lax.linalg.tridiagonal_solve(sub_diag, main_diag, super_diag, right_side)  50.3 us
    div x2, other arithmetic, reduced_solve(): solved[pivot_index] = running / matrix[pivot_index, pivot_index]  44.4 us
    ppermute x18, starting transfers between devices, with_halo(): lax.ppermute(lax.slice_in_dim(block, 0, width, axis=dim), axis, backward)  30.8 us
    sub x2, other arithmetic, cable_solve(): lax.linalg.tridiagonal_solve(sub_diag, main_diag, super_diag, right_side)  27.7 us
    div x4, other arithmetic, on_device(): lax.linalg.tridiagonal_solve(sub_diag, main_diag, super_diag, unit_columns)  26.8 us
  transfers between devices with their start and end apart: 39, of which 6 were waited for; matrix products, arithmetic and copies ran while one was open for 54% of the time, Pallas kernels for 0%

commit v1 on v0

v1 whole, which is shorter than its diff:
```python
import math

import jax
import jax.numpy as jnp
import numpy as np
from jax import lax
from jax.experimental import pallas as pl
from jax.experimental.pallas import tpu as pltpu
from jax.sharding import PartitionSpec as P

STEPS = 2
SWEEPS = 4
NPC = 2

time_step = 0.5
conductance = 2000.0
amplitude = 200.0
band_half = 4
low_bound = 0.5
high_bound = 14.0

MESH = pl.DeviceIdType.MESH
HIGH = lax.Precision.HIGHEST
F32 = jnp.float32
BF16 = jnp.bfloat16

N_FIB, N_LEN, N_EMG = 8, 4, 4
GROUPS = N_FIB * N_EMG
STATES = 57
ROWS = 64
NODES = 64
FIB = 128
BINS = NODES // NPC
BY, BZ = 8, 128
SLOT_ROWS = 4
CAPACITY = 12
FACE_ROWS = 112


def cable_tables():
    total = NODES * N_LEN
    theta = math.acosh(1.0 + 0.5 / conductance)
    scale = conductance * math.sinh(theta) * math.sinh(total * theta)
    u = np.array([math.cosh((i + 0.5) * theta) for i in range(total)])
    v = np.array([math.cosh((total - 0.5 - i) * theta) / scale for i in range(total)])
    index = np.arange(NODES)
    local = np.zeros((N_LEN, NODES + 8, NODES))
    far = np.zeros((N_LEN, NODES, 8 * N_LEN))
    for shard in range(N_LEN):
        us, vs = u[shard * NODES :][:NODES], v[shard * NODES :][:NODES]
        low = index[:, None] <= index[None, :]
        local[shard, :NODES] = np.where(low, us[:, None] * vs[None, :], vs[:, None] * us[None, :])
        local[shard, NODES] = us
        local[shard, NODES + 1] = vs
        for other in range(N_LEN):
            if other < shard:
                far[shard, :, 8 * other] = vs
            if other > shard:
                far[shard, :, 8 * other + 1] = us
    return jnp.asarray(local, F32), jnp.asarray(far, F32)


def iota(shape, axis):
    return lax.broadcasted_iota(jnp.int32, shape, axis)


def split(values):
    high = values.astype(BF16)
    return high, (values - high.astype(F32)).astype(BF16)


def dot(a, b):
    return jnp.dot(a, b, preferred_element_type=F32)


def dot_high(a, b):
    return jnp.dot(a, b, preferred_element_type=F32, precision=HIGH)


def dot_t(a, b, precision=None):
    return lax.dot_general(
        a, b, (((1,), (1,)), ((), ())), preferred_element_type=F32, precision=precision
    )


def dot_tl(a, b, precision=None):
    return lax.dot_general(
        a, b, (((0,), (0,)), ((), ())), preferred_element_type=F32, precision=precision
    )


def kernel(
    states_hbm, volt_ref, coup_ref, decay_ref, gain_ref, wts_ref, home_ref, cell_ref, mu_ref,
    stim_ref, tissue_ref, local_ref, far_ref,
    states_out, volt_out, pot_out,
    s_in, s_work, s_new, lhs_ref, keep_ref, gain_b, wts_b, cur_ref, v1_ref, hot_ref, sel_ref,
    cell_send, cell_recv, row_send, row_recv, end_send, end_recv, face_send, face_recv,
    d_ref, r_ref, x_ref, hy_ref, hz_ref,
    in_sem, out_sem, a2a_send, a2a_recv, len_send, len_recv, face_ssem, face_rsem,
):
    fib, shard, emg = lax.axis_index("fib"), lax.axis_index("len"), lax.axis_index("emg")
    me = fib * N_EMG + emg

    quarter = NODES // 4
    loads = []
    for part in range(4):
        window = pl.ds(part * quarter, quarter)
        copy = pltpu.make_async_copy(
            states_hbm.at[:, window, :], s_in.at[pl.ds(0, STATES), window, :], in_sem.at[part]
        )
        copy.start()
        loads.append(copy)

    barrier = pltpu.get_barrier_semaphore()

    def peer(step):
        other = lax.rem(me + step, GROUPS)
        return {"fib": other // N_EMG, "len": shard, "emg": lax.rem(other, N_EMG)}, other

    def greet(step, _):
        device, _other = peer(step)
        pl.semaphore_signal(barrier, inc=1, device_id=device, device_id_type=MESH)
        return 0

    lax.fori_loop(1, GROUPS, greet, 0)
    for step in range(1, N_LEN):
        other = lax.rem(shard + step, N_LEN)
        pl.semaphore_signal(
            barrier, inc=1, device_id={"fib": fib, "len": other, "emg": emg}, device_id_type=MESH
        )

    def column(row):
        wide = row.shape[1]
        picked = jnp.where(iota((ROWS, wide), 0) == iota((ROWS, wide), 1), row, 0.0)
        return dot_high(picked, jnp.ones((wide, FIB), F32))

    keep_ref[...] = 1.0 - time_step * column(decay_ref[...])
    gain_b[...] = column(gain_ref[...])
    wts_b[...] = column(wts_ref[...])
    spread = (iota((STATES, 3 * ROWS), 0) == lax.rem(iota((STATES, 3 * ROWS), 1), ROWS)).astype(F32)
    tiled = dot_high(coup_ref[...], spread)
    tiled = jnp.concatenate([tiled, jnp.zeros((ROWS - STATES, 3 * ROWS), F32)], axis=0)
    weights = dot_high(wts_ref[...], spread)
    tiled = jnp.where(iota((ROWS, 3 * ROWS), 0) == STATES, weights, tiled)
    high, low = split(tiled)
    lhs_ref[...] = jnp.where(iota((ROWS, 3 * ROWS), 1) < 2 * ROWS, high.astype(F32), low.astype(F32)).astype(BF16)

    unit_hot = (iota((FIB, FIB), 0) == mu_ref[...]).astype(F32)
    stim_row = jnp.concatenate(
        [stim_ref[...].astype(F32), jnp.zeros((1, FIB - stim_ref.shape[1]), F32)], axis=1
    )
    fire = dot(stim_row.astype(BF16), unit_hot.astype(BF16))

    home = home_ref[...]
    member = (iota((GROUPS, FIB), 0) == home).astype(F32)
    before = (iota((FIB, FIB), 0) < iota((FIB, FIB), 1)).astype(BF16)
    earlier = dot(member.astype(BF16), before)
    rank = jnp.sum(earlier * member, axis=0, keepdims=True).astype(jnp.int32)
    slot = home * CAPACITY + rank
    packed = GROUPS * SLOT_ROWS
    row_id = iota((packed, FIB), 0)
    in_brick = lax.rem(row_id, SLOT_ROWS)
    first_slot = (row_id // SLOT_ROWS) * CAPACITY + 4 * in_brick
    for q in range(4):
        chosen = (slot == first_slot + q) & (in_brick < CAPACITY // 4)
        sel_ref[:, q * FIB : (q + 1) * FIB] = chosen.astype(F32).astype(BF16)

    def pack(values):
        blank = jnp.zeros((BINS, FIB), BF16)
        total = None
        for part in split(values):
            block = jnp.concatenate(
                [
                    jnp.concatenate([part if q == row else blank for q in range(4)], axis=1)
                    for row in range(4)
                ],
                axis=0,
            )
            term = dot_t(sel_ref[...], block)
            total = term if total is None else total + term
        return total.reshape(GROUPS, SLOT_ROWS, FIB)

    def exchange(source, target, slot_index):
        def send(step, _):
            device, other = peer(step)
            pltpu.make_async_remote_copy(
                source.at[other], target.at[me], a2a_send.at[slot_index], a2a_recv.at[slot_index],
                device_id=device, device_id_type=MESH,
            ).start()
            return 0

        lax.fori_loop(1, GROUPS, send, 0)
        target[me] = source[me]

    def exchange_wait(target, slot_index):
        whole = target.at[pl.ds(0, GROUPS - 1)]
        pltpu.make_async_copy(whole, whole, a2a_recv.at[slot_index]).wait()

    def exchange_sent(source, slot_index):
        whole = source.at[pl.ds(0, GROUPS - 1)]
        pltpu.make_async_copy(whole, whole, a2a_send.at[slot_index]).wait()

    cell_row = jnp.broadcast_to(cell_ref[...].astype(F32), (BINS, FIB))
    cell_send[...] = pack(cell_row)
    pl.semaphore_wait(barrier, GROUPS - 1 + N_LEN - 1)
    exchange(cell_send, cell_recv, 0)

    s_flat = s_in.reshape(ROWS * NODES, FIB)
    s_in[pl.ds(STATES, ROWS - STATES)] = jnp.zeros((ROWS - STATES, NODES, FIB), F32)

    def stacked(values):
        high, low = split(values)
        return jnp.concatenate([high, low, high], axis=0)

    def twice(values):
        return jnp.concatenate([values, values], axis=1)

    def first_pair(pair, _):
        node = 2 * pair
        old = jnp.concatenate(
            [s_flat[pl.ds(node + k, ROWS, stride=NODES), :] for k in range(2)], axis=1
        )
        volts = jnp.concatenate([volt_ref[pl.ds(node + k, 1), :] for k in range(2)], axis=1)
        gain = twice(gain_b[...])
        drive = dot(lhs_ref[...], stacked(old)) + gain * volts
        new = twice(keep_ref[...]) * old + time_step * jnp.tanh(drive)
        new = jnp.where(iota(new.shape, 0) < STATES, new, 0.0)
        after = dot(lhs_ref[...], stacked(new))
        for k in range(2):
            lanes = slice(k * FIB, (k + 1) * FIB)
            s_work[node + k] = new[:, lanes]
            s_new[node + k] = after[:, lanes]
            cur_ref[pl.ds(node + k, 1), :] = after[STATES : STATES + 1, lanes]
        return 0

    for part in range(4):
        loads[part].wait()
        lax.fori_loop(part * (quarter // 2), (part + 1) * (quarter // 2), first_pair, 0, unroll=2)

    node_id = shard * NODES + iota((NODES, FIB), 0)
    total_nodes = NODES * N_LEN
    band = (node_id >= total_nodes // 2 - band_half) & (node_id < total_nodes // 2 + band_half)

    def cable_begin(step, volts):
        active = (fire == float(step)).astype(F32)
        pulse = jnp.where(band, amplitude * active, 0.0)
        right = volts + time_step * (pulse - cur_ref[...])
        both = dot_high(local_ref[shard], right)
        end_send[step] = both[NODES:]
        for other_step in range(1, N_LEN):
            other = lax.rem(shard + other_step, N_LEN)
            pltpu.make_async_remote_copy(
                end_send.at[step], end_recv.at[step, shard], len_send.at[step], len_recv.at[step],
                device_id={"fib": fib, "len": other, "emg": emg}, device_id_type=MESH,
            ).start()
        end_recv[step, shard] = jnp.zeros((8, FIB), F32)
        return both[:NODES]

    def cable_end(step, local):
        whole = end_recv.at[step, pl.ds(0, N_LEN - 1)]
        pltpu.make_async_copy(whole, whole, len_recv.at[step]).wait()
        far = end_recv[step].reshape(8 * N_LEN, FIB)
        return local + dot_high(far_ref[shard], far)

    def binned():
        first = cur_ref[pl.ds(0, BINS, stride=2), :]
        second = cur_ref[pl.ds(1, BINS, stride=2), :]
        return first + second

    local = cable_begin(0, volt_ref[...])
    row_send[0] = pack(binned())
    exchange(row_send.at[0], row_recv.at[0], 1)

    exchange_wait(cell_recv, 0)
    cells = cell_recv[...].reshape(packed, FIB)
    for q in range(4):
        column_q = cells[:, q * BINS : q * BINS + 1].astype(jnp.int32)
        for y in range(BY):
            hot = (column_q == iota((packed, BZ), 1) + y * BZ).astype(F32).astype(BF16)
            hot_ref[q * packed : (q + 1) * packed, y * BZ : (y + 1) * BZ] = hot

    v1_ref[...] = cable_end(0, local)

    o_flat = s_in.reshape(ROWS * NODES, FIB)

    def second_pair(node, _):
        drive = s_new[node] + gain_b[...] * v1_ref[pl.ds(node, 1), :]
        new = keep_ref[...] * s_work[node] + time_step * jnp.tanh(drive)
        o_flat[pl.ds(node, ROWS, stride=NODES), :] = new
        cur_ref[pl.ds(node, 1), :] = jnp.sum(wts_b[...] * new, axis=0, keepdims=True)
        return 0

    stores = []
    for part in range(4):
        lax.fori_loop(part * quarter, (part + 1) * quarter, second_pair, 0, unroll=2)
        window = pl.ds(part * quarter, quarter)
        copy = pltpu.make_async_copy(
            s_in.at[pl.ds(0, STATES), window, :], states_out.at[:, window, :], out_sem.at[part]
        )
        copy.start()
        stores.append(copy)

    row_send[1] = pack(binned())
    exchange(row_send.at[1], row_recv.at[1], 2)
    local = cable_begin(1, v1_ref[...])

    middle = 0.5 * (high_bound + low_bound)
    spread_width = 0.5 * (high_bound - low_bound)
    ratio = middle / spread_width
    lane = iota((BY, BZ), 1)
    sub = iota((BY, BZ), 0)

    def scatter(step):
        exchange_wait(row_recv.at[step], 1 + step)
        rows = row_recv[step].reshape(packed, FIB)
        turned = rows.T
        wide = jnp.concatenate([turned[q * BINS : (q + 1) * BINS] for q in range(4)], axis=1)
        both = dot(jnp.concatenate(split(wide), axis=0), hot_ref[...])
        source = both[:BINS] + both[BINS:]
        flat = r_ref.at[step].reshape(BINS * BY, BZ)
        for y in range(BY):
            flat[pl.ds(y, BINS, stride=BY), :] = source[:, y * BZ : (y + 1) * BZ]
        first = r_ref[step] * (1.0 / middle)
        d_ref[step, pl.ds(1, BINS)] = first
        x_ref[step] = first

    def faces(step, sweep):
        send = face_send.at[step, sweep]
        recv = face_recv.at[step, sweep]
        flat = d_ref.at[step].reshape((BINS + 2) * BY, BZ)
        send[0:32, :] = flat[pl.ds(BY, BINS, stride=BY), :]
        send[32:64, :] = flat[pl.ds(2 * BY - 1, BINS, stride=BY), :]
        send[64:72, :] = flat[BY : 2 * BY, :]
        send[72:80, :] = flat[BINS * BY : (BINS + 1) * BY, :]
        pick = (iota((8, BZ), 1) == (BZ - 1) * iota((8, BZ), 0)).astype(F32)
        side = dot_t(pick, flat[BY : (BINS + 1) * BY, :], HIGH)
        send[80:88, :] = side[:, :BZ]
        send[88:96, :] = side[:, BZ:]
        up, down = lax.rem(fib + 1, N_FIB), lax.rem(fib + N_FIB - 1, N_FIB)
        right, left = lax.rem(shard + 1, N_LEN), lax.rem(shard + N_LEN - 1, N_LEN)
        front, back = lax.rem(emg + 1, N_EMG), lax.rem(emg + N_EMG - 1, N_EMG)
        plan = (
            (0, 32, 32, {"fib": down, "len": shard, "emg": emg}),
            (32, 0, 32, {"fib": up, "len": shard, "emg": emg}),
            (64, 72, 8, {"fib": fib, "len": left, "emg": emg}),
            (72, 64, 8, {"fib": fib, "len": right, "emg": emg}),
            (80, 96, 16, {"fib": fib, "len": shard, "emg": back}),
            (80, 80, 16, {"fib": fib, "len": shard, "emg": front}),
        )
        for source, target, height, device in plan:
            pltpu.make_async_remote_copy(
                send.at[pl.ds(source, height)], recv.at[pl.ds(target, height)],
                face_ssem.at[step, sweep], face_rsem.at[step, sweep],
                device_id=device, device_id_type=MESH,
            ).start()

    def sweep_on(step, sweep, weight_now, weight_next):
        recv = face_recv.at[step, sweep]
        pltpu.make_async_copy(recv, recv, face_rsem.at[step, sweep]).wait()

        def unless(edge):
            return jnp.where(edge, 0.0, 1.0).astype(F32)

        d_ref[step, 0] = recv[64:72, :] * unless(shard == 0)
        d_ref[step, BINS + 1] = recv[72:80, :] * unless(shard == N_LEN - 1)
        hy_flat = hy_ref.reshape(BINS * BY, BZ)
        hy_flat[pl.ds(0, BINS, stride=BY), :] = recv[0:32, :] * unless(fib == 0)
        hy_flat[pl.ds(BY - 1, BINS, stride=BY), :] = recv[32:64, :] * unless(fib == N_FIB - 1)
        low_side = jnp.concatenate([recv[80:88, :], recv[88:96, :]], axis=1)
        high_side = jnp.concatenate([recv[96:104, :], recv[104:112, :]], axis=1)
        row, col = iota((16, BZ), 0), iota((16, BZ), 1)
        inject = jnp.where((row == 1) & (col == 0), unless(emg == 0), 0.0)
        inject = inject + jnp.where((row == 8) & (col == BZ - 1), unless(emg == N_EMG - 1), 0.0)
        hz_ref[...] = dot_tl(jnp.concatenate([low_side, high_side], axis=0), inject, HIGH).reshape(
            BINS, BY, BZ
        )
        keep, gain = weight_next * weight_now, 2.0 * weight_next / spread_width

        def slab(x, previous):
            here = d_ref[step, x + 1]
            beside = previous + d_ref[step, x + 2] + hy_ref[x] + hz_ref[x]
            beside = beside + jnp.where(sub == 0, 0.0, pltpu.roll(here, 1, 0))
            beside = beside + jnp.where(sub == BY - 1, 0.0, pltpu.roll(here, BY - 1, 0))
            beside = beside + jnp.where(lane == 0, 0.0, pltpu.roll(here, 1, 1))
            beside = beside + jnp.where(lane == BZ - 1, 0.0, pltpu.roll(here, BZ - 1, 1))
            rest = r_ref[step, x] - ((6.0 + tissue_ref[x]) * here - beside)
            after = keep * here + gain * rest
            r_ref[step, x] = rest
            d_ref[step, x + 1] = after
            if sweep == SWEEPS - 2:
                pot_out[step, x] = x_ref[step, x] + after
            else:
                x_ref[step, x] = x_ref[step, x] + after
            return here

        lax.fori_loop(0, BINS, slab, d_ref[step, 0], unroll=4)

    weight = [1.0 / ratio]
    for _ in range(SWEEPS - 1):
        weight.append(1.0 / (2.0 * ratio - weight[-1]))

    def advance(step, sweep):
        sweep_on(step, sweep, weight[sweep], weight[sweep + 1])
        if sweep < SWEEPS - 2:
            faces(step, sweep + 1)

    scatter(0)
    faces(0, 0)
    volt_out[...] = cable_end(1, local)
    advance(0, 0)
    scatter(1)
    faces(1, 0)
    advance(0, 1)
    advance(1, 0)
    advance(0, 2)
    advance(1, 1)
    advance(1, 2)

    for copy in stores:
        copy.wait()
    exchange_sent(cell_send, 0)
    for step in range(STEPS):
        exchange_sent(row_send.at[step], 1 + step)
        whole = end_recv.at[step, pl.ds(0, N_LEN - 1)]
        pltpu.make_async_copy(whole, whole, len_send.at[step]).wait()
        for sweep in range(SWEEPS - 1):
            sent = face_send.at[step, sweep]
            pltpu.make_async_copy(sent, sent, face_ssem.at[step, sweep]).wait()


def on_device(
    states, voltage, coupling, decay_rates, volt_gain, current_weights,
    fibre_home, cross_cell, motor_unit, stim_step, tissue,
):
    local, far = cable_tables()
    vmem = pl.BlockSpec(memory_space=pltpu.VMEM)
    hbm = pl.BlockSpec(memory_space=pl.ANY)
    sweeps = SWEEPS - 1
    return pl.pallas_call(
        kernel,
        out_shape=(
            jax.ShapeDtypeStruct(states.shape, F32),
            jax.ShapeDtypeStruct(voltage.shape, F32),
            jax.ShapeDtypeStruct((STEPS, *tissue.shape), F32),
        ),
        in_specs=[hbm] + [vmem] * 12,
        out_specs=(hbm, vmem, vmem),
        scratch_shapes=[
            pltpu.VMEM((ROWS, NODES, FIB), F32),
            pltpu.VMEM((NODES, ROWS, FIB), F32),
            pltpu.VMEM((NODES, ROWS, FIB), F32),
            pltpu.VMEM((ROWS, 3 * ROWS), BF16),
            pltpu.VMEM((ROWS, FIB), F32),
            pltpu.VMEM((ROWS, FIB), F32),
            pltpu.VMEM((ROWS, FIB), F32),
            pltpu.VMEM((NODES, FIB), F32),
            pltpu.VMEM((NODES, FIB), F32),
            pltpu.VMEM((4 * GROUPS * SLOT_ROWS, BY * BZ), BF16),
            pltpu.VMEM((GROUPS * SLOT_ROWS, 4 * FIB), BF16),
            pltpu.VMEM((GROUPS, SLOT_ROWS, FIB), F32),
            pltpu.VMEM((GROUPS, SLOT_ROWS, FIB), F32),
            pltpu.VMEM((STEPS, GROUPS, SLOT_ROWS, FIB), F32),
            pltpu.VMEM((STEPS, GROUPS, SLOT_ROWS, FIB), F32),
            pltpu.VMEM((STEPS, 8, FIB), F32),
            pltpu.VMEM((STEPS, N_LEN, 8, FIB), F32),
            pltpu.VMEM((STEPS, sweeps, FACE_ROWS, FIB), F32),
            pltpu.VMEM((STEPS, sweeps, FACE_ROWS, FIB), F32),
            pltpu.VMEM((STEPS, BINS + 2, BY, BZ), F32),
            pltpu.VMEM((STEPS, BINS, BY, BZ), F32),
            pltpu.VMEM((STEPS, BINS, BY, BZ), F32),
            pltpu.VMEM((BINS, BY, BZ), F32),
            pltpu.VMEM((BINS, BY, BZ), F32),
            pltpu.SemaphoreType.DMA((4,)),
            pltpu.SemaphoreType.DMA((4,)),
            pltpu.SemaphoreType.DMA((3,)),
            pltpu.SemaphoreType.DMA((3,)),
            pltpu.SemaphoreType.DMA((STEPS,)),
            pltpu.SemaphoreType.DMA((STEPS,)),
            pltpu.SemaphoreType.DMA((STEPS, sweeps)),
            pltpu.SemaphoreType.DMA((STEPS, sweeps)),
        ],
        compiler_params=pltpu.CompilerParams(collective_id=0, has_side_effects=True),
    )(
        states, voltage, coupling, decay_rates.reshape(1, -1), volt_gain.reshape(1, -1),
        current_weights.reshape(1, -1), fibre_home.reshape(1, -1), cross_cell.reshape(1, -1),
        motor_unit.reshape(1, -1), stim_step.reshape(1, -1), tissue, local, far,
    )


def solution(mesh):
    return jax.shard_map(
        on_device,
        mesh=mesh,
        in_specs=(
            P(None, "len", ("fib", "emg")),
            P("len", ("fib", "emg")),
            P(),
            P(),
            P(),
            P(),
            P(("fib", "emg"), None),
            P(("fib", "emg")),
            P(("fib", "emg")),
            P(),
            P("len", "fib", "emg"),
        ),
        out_specs=(
            P(None, "len", ("fib", "emg")),
            P("len", ("fib", "emg")),
            P(None, "len", "fib", "emg"),
        ),
        check_vma=False,
    )
```

time: 756 us -> 49.9 us (0.07); the launches traced: 741 us -> 49 us
  other arithmetic: 341 us -> 0 us
  between operations: 168 us -> 0.66 us
  starting transfers between devices: 123 us -> 0 us
  local copies, waits for them, and re-layouts: 56 us -> 4.34 us
  Pallas kernels: 0 us -> 44 us
  blocking collectives: 20.7 us -> 0 us
  waiting for transfers between devices: 20.6 us -> 0 us
  matrix products: 12 us -> 0 us
    broadcast_in_dim x32 -> x0, other arithmetic: 146 us -> none  [the longest x21 94.2 us: cable_solve(): lax.linalg.tridiagonal_solve(sub_diag, main_diag, super_diag, right_side)]
    div x10 -> x0, other arithmetic: 122 us -> none  [the longest x2 50.3 us: cable_solve(): lax.linalg.tridiagonal_solve(sub_diag, main_diag, super_diag, right_side)]
    ppermute x36 -> x0, starting transfers between devices: 95.9 us -> none  [the longest x18 65.1 us: with_halo(): lax.ppermute(lax.slice_in_dim(block, block.shape[dim] - width, None, axis...]
    pallas_call x0 -> x1, Pallas kernels: none -> 44 us  [on_device(): pl.pallas_call(kernel, out_shape=(jax.ShapeDtypeStruct(states.shape, F32)...]
    sub x4 -> x0, other arithmetic: 41.7 us -> none  [the longest x2 27.7 us: cable_solve(): lax.linalg.tridiagonal_solve(sub_diag, main_diag, super_diag, right_side)]
    slice x62 -> x0, local copies, waits for them, and re-layouts: 33 us -> none  [the longest x28 18 us: reduced_solve(): factor = matrix[row_index, pivot_index] / matrix[pivot_index, pivot_index]]
    all_to_all x3 -> x0, starting transfers between devices: 27.1 us -> none  [the longest x2 17.5 us: on_device(): lax.all_to_all(rows_sent, ('fib', 'emg'), split_axis=0, concat_axis=0, ti...]
    ppermute x36 -> x0, waiting for transfers between devices: 14.5 us -> none  [the longest x18 12.7 us: with_halo(): lax.ppermute(lax.slice_in_dim(block, 0, width, axis=dim), axis, backward)]
  transfers between devices with their start and end apart: 39 -> 0, of which waited for: 6 -> 0; matrix products, arithmetic and copies ran while one was open for 54% -> 0% of each run, Pallas kernels for 0% -> 0%
where the time goes in v1:
time: 49.9 us; the launch traced here: 49 us
  Pallas kernels  44 us (88%)
  local copies, waits for them, and re-layouts  4.34 us (9%)
  between operations  0.66 us (1%)
    pallas_call x1, Pallas kernels, on_device(): pl.pallas_call(kernel, out_shape=(jax.ShapeDtypeStruct(states.shape, F32)...  44 us
    unnamed x7, local copies, waits for them, and re-layouts  4.34 us

profile of v1, /device:TPU:1, one launch (start us, length us, event | category | flops | bytes accessed | tf_op | source)
XLA Modules:
  0.0 49.0 jit_solution(3763201266433006809)
XLA Ops:
  0.6 44.0 %shard_map.148 = (f32[57,64,128]{2,1,0:T(8,128)}, f32[64,128]{1,0:T(8,128)}, f32[2,32,8,128]{3,2,1,0:T(8,128)}) custom-call(f32[57,64,128]{2,1,0:T(8,128)} %states_hbm.1, f32[64,128]{1,0:T(8,128)} %volt_ref.1, f32[57,57]{1,0:T(8,128)} %coup_ref.1, f32[1,57]{1,0:T(1,128)} %bitcast.7, f32[1,57]{1,0:T(1,128)} %bitcast.8, f32[1,57]{1,0:T(1,128)} %bitcast.9, ...), custom_call_target="tpu_custom_call" | custom-call | tf_op jit(solution)/shard_map/pallas_call | solution.py:439
  44.6 0.0 copy-start.1
  44.6 0.0 copy-start
  44.6 3.0 %copy.19 = f32[57,64,128]{2,1,0:T(8,128)} copy(f32[57,64,128]{2,1,0:T(8,128)} %get-tuple-element.6) | data formatting | bytes 3735552
  47.7 0.0 copy-done.1
  47.7 0.6 %copy.20 = f32[64,128]{1,0:T(8,128)} copy(f32[64,128]{1,0:T(8,128)S(1)} %copy-done.1) | data formatting | bytes 65536
  48.3 0.0 copy-done
  48.3 0.7 %copy.21 = f32[2,32,8,128]{3,2,1,0:T(8,128)} copy(f32[2,32,8,128]{3,2,1,0:T(8,128)S(1)} %copy-done) | data formatting | bytes 524288
Async XLA Ops:
  44.6 3.0 %copy-start.1 = (f32[64,128]{1,0:T(8,128)S(1)}, f32[64,128]{1,0:T(8,128)}, u32[]{:S(2)}) copy-start(f32[64,128]{1,0:T(8,128)} %get-tuple-element.7) | copy-start | bytes 98308
  44.6 3.6 %copy-start = (f32[2,32,8,128]{3,2,1,0:T(8,128)S(1)}, f32[2,32,8,128]{3,2,1,0:T(8,128)}, u32[]{:S(2)}) copy-start(f32[2,32,8,128]{3,2,1,0:T(8,128)} %get-tuple-element.8) | copy-start | bytes 786436

commit v2 on v1

--- a/solution.py
+++ b/solution.py
@@ -35,6 +35,7 @@
 SLOT_ROWS = 4
 CAPACITY = 12
 FACE_ROWS = 112
+VMEM_LIMIT = 24 << 20
 
 
 def cable_tables():
@@ -90,18 +91,31 @@
 
 
 def kernel(
-    states_hbm, volt_ref, coup_ref, decay_ref, gain_ref, wts_ref, home_ref, cell_ref, mu_ref,
+    states_hbm, volt_hbm, coup_hbm, decay_hbm, gain_hbm, wts_hbm, home_hbm, cell_hbm, mu_hbm,
+    stim_hbm, tissue_hbm, local_hbm, far_hbm,
+    states_out, volt_out, pot_out,
+    volt_ref, coup_ref, decay_ref, gain_ref, wts_ref, home_ref, cell_ref, mu_ref,
     stim_ref, tissue_ref, local_ref, far_ref,
-    states_out, volt_out, pot_out,
     s_in, s_work, s_new, lhs_ref, keep_ref, gain_b, wts_b, cur_ref, v1_ref, hot_ref, sel_ref,
     cell_send, cell_recv, row_send, row_recv, end_send, end_recv, face_send, face_recv,
     d_ref, r_ref, x_ref, hy_ref, hz_ref,
-    in_sem, out_sem, a2a_send, a2a_recv, len_send, len_recv, face_ssem, face_rsem,
+    in_sem, small_sem, a2a_send, a2a_recv, len_send, len_recv, face_ssem, face_rsem,
 ):
     fib, shard, emg = lax.axis_index("fib"), lax.axis_index("len"), lax.axis_index("emg")
     me = fib * N_EMG + emg
 
     quarter = NODES // 4
+    smalls = [
+        pltpu.make_async_copy(source, target, small_sem.at[number])
+        for number, (source, target) in enumerate((
+            (coup_hbm, coup_ref), (decay_hbm, decay_ref), (gain_hbm, gain_ref), (wts_hbm, wts_ref),
+            (home_hbm, home_ref), (cell_hbm, cell_ref), (mu_hbm, mu_ref), (stim_hbm, stim_ref),
+            (volt_hbm, volt_ref), (local_hbm, local_ref), (far_hbm, far_ref),
+            (tissue_hbm, tissue_ref),
+        ))
+    ]
+    for copy in smalls:
+        copy.start()
     loads = []
     for part in range(4):
         window = pl.ds(part * quarter, quarter)
@@ -134,6 +148,8 @@
         picked = jnp.where(iota((ROWS, wide), 0) == iota((ROWS, wide), 1), row, 0.0)
         return dot_high(picked, jnp.ones((wide, FIB), F32))
 
+    for copy in smalls[:8]:
+        copy.wait()
     keep_ref[...] = 1.0 - time_step * column(decay_ref[...])
     gain_b[...] = column(gain_ref[...])
     wts_b[...] = column(wts_ref[...])
@@ -202,8 +218,9 @@
 
     cell_row = jnp.broadcast_to(cell_ref[...].astype(F32), (BINS, FIB))
     cell_send[...] = pack(cell_row)
-    pl.semaphore_wait(barrier, GROUPS - 1 + N_LEN - 1)
-    exchange(cell_send, cell_recv, 0)
+
+    for copy in smalls[8:]:
+        copy.wait()
 
     s_flat = s_in.reshape(ROWS * NODES, FIB)
     s_in[pl.ds(STATES, ROWS - STATES)] = jnp.zeros((ROWS - STATES, NODES, FIB), F32)
@@ -224,7 +241,6 @@
         gain = twice(gain_b[...])
         drive = dot(lhs_ref[...], stacked(old)) + gain * volts
         new = twice(keep_ref[...]) * old + time_step * jnp.tanh(drive)
-        new = jnp.where(iota(new.shape, 0) < STATES, new, 0.0)
         after = dot(lhs_ref[...], stacked(new))
         for k in range(2):
             lanes = slice(k * FIB, (k + 1) * FIB)
@@ -235,7 +251,10 @@
 
     for part in range(4):
         loads[part].wait()
-        lax.fori_loop(part * (quarter // 2), (part + 1) * (quarter // 2), first_pair, 0, unroll=2)
+        lax.fori_loop(part * (quarter // 2), (part + 1) * (quarter // 2), first_pair, 0, unroll=8)
+        if part == 1:
+            pl.semaphore_wait(barrier, GROUPS - 1 + N_LEN - 1)
+            exchange(cell_send, cell_recv, 0)
 
     node_id = shard * NODES + iota((NODES, FIB), 0)
     total_nodes = NODES * N_LEN
@@ -278,31 +297,6 @@
         for y in range(BY):
             hot = (column_q == iota((packed, BZ), 1) + y * BZ).astype(F32).astype(BF16)
             hot_ref[q * packed : (q + 1) * packed, y * BZ : (y + 1) * BZ] = hot
-
-    v1_ref[...] = cable_end(0, local)
-
-    o_flat = s_in.reshape(ROWS * NODES, FIB)
-
-    def second_pair(node, _):
-        drive = s_new[node] + gain_b[...] * v1_ref[pl.ds(node, 1), :]
-        new = keep_ref[...] * s_work[node] + time_step * jnp.tanh(drive)
-        o_flat[pl.ds(node, ROWS, stride=NODES), :] = new
-        cur_ref[pl.ds(node, 1), :] = jnp.sum(wts_b[...] * new, axis=0, keepdims=True)
-        return 0
-
-    stores = []
-    for part in range(4):
-        lax.fori_loop(part * quarter, (part + 1) * quarter, second_pair, 0, unroll=2)
-        window = pl.ds(part * quarter, quarter)
-        copy = pltpu.make_async_copy(
-            s_in.at[pl.ds(0, STATES), window, :], states_out.at[:, window, :], out_sem.at[part]
-        )
-        copy.start()
-        stores.append(copy)
-
-    row_send[1] = pack(binned())
-    exchange(row_send.at[1], row_recv.at[1], 2)
-    local = cable_begin(1, v1_ref[...])
 
     middle = 0.5 * (high_bound + low_bound)
     spread_width = 0.5 * (high_bound - low_bound)
@@ -393,7 +387,7 @@
                 x_ref[step, x] = x_ref[step, x] + after
             return here
 
-        lax.fori_loop(0, BINS, slab, d_ref[step, 0], unroll=4)
+        lax.fori_loop(0, BINS, slab, d_ref[step, 0], unroll=16)
 
     weight = [1.0 / ratio]
     for _ in range(SWEEPS - 1):
@@ -404,10 +398,28 @@
         if sweep < SWEEPS - 2:
             faces(step, sweep + 1)
 
+    v1_ref[...] = cable_end(0, local)
+
+    o_flat = states_out.reshape(STATES * NODES, FIB)
+
+    def second(node, _):
+        drive = s_new[node] + gain_b[...] * v1_ref[pl.ds(node, 1), :]
+        new = keep_ref[...] * s_work[node] + time_step * jnp.tanh(drive)
+        o_flat[pl.ds(node, STATES, stride=NODES), :] = new[:STATES]
+        cur_ref[pl.ds(node, 1), :] = jnp.sum(wts_b[...] * new, axis=0, keepdims=True)
+        return 0
+
+    lax.fori_loop(0, NODES // 2, second, 0, unroll=8)
     scatter(0)
     faces(0, 0)
+    lax.fori_loop(NODES // 2, NODES, second, 0, unroll=8)
+
+    row_send[1] = pack(binned())
+    exchange(row_send.at[1], row_recv.at[1], 2)
+    local = cable_begin(1, v1_ref[...])
+
+    advance(0, 0)
     volt_out[...] = cable_end(1, local)
-    advance(0, 0)
     scatter(1)
     faces(1, 0)
     advance(0, 1)
@@ -416,8 +428,6 @@
     advance(1, 1)
     advance(1, 2)
 
-    for copy in stores:
-        copy.wait()
     exchange_sent(cell_send, 0)
     for step in range(STEPS):
         exchange_sent(row_send.at[step], 1 + step)
@@ -428,24 +438,54 @@
             pltpu.make_async_copy(sent, sent, face_ssem.at[step, sweep]).wait()
 
 
+def write_out(states, voltage, potential, states_out, voltage_out, potential_out, sem):
+    cuts = (0, 15, 29, 43, STATES)
+    copies = [
+        pltpu.make_async_copy(
+            states.at[pl.ds(cuts[k], cuts[k + 1] - cuts[k])],
+            states_out.at[pl.ds(cuts[k], cuts[k + 1] - cuts[k])],
+            sem.at[k],
+        )
+        for k in range(4)
+    ]
+    copies.append(pltpu.make_async_copy(potential, potential_out, sem.at[4]))
+    copies.append(pltpu.make_async_copy(voltage, voltage_out, sem.at[5]))
+    for copy in copies:
+        copy.start()
+    for copy in copies:
+        copy.wait()
+
+
 def on_device(
     states, voltage, coupling, decay_rates, volt_gain, current_weights,
     fibre_home, cross_cell, motor_unit, stim_step, tissue,
 ):
     local, far = cable_tables()
     vmem = pl.BlockSpec(memory_space=pltpu.VMEM)
-    hbm = pl.BlockSpec(memory_space=pl.ANY)
+    hbm = pl.BlockSpec(memory_space=pltpu.HBM)
     sweeps = SWEEPS - 1
-    return pl.pallas_call(
+    outputs = pl.pallas_call(
         kernel,
         out_shape=(
             jax.ShapeDtypeStruct(states.shape, F32),
             jax.ShapeDtypeStruct(voltage.shape, F32),
             jax.ShapeDtypeStruct((STEPS, *tissue.shape), F32),
         ),
-        in_specs=[hbm] + [vmem] * 12,
-        out_specs=(hbm, vmem, vmem),
+        in_specs=[hbm] * 13,
+        out_specs=(vmem, vmem, vmem),
         scratch_shapes=[
+            pltpu.VMEM(voltage.shape, F32),
+            pltpu.VMEM(coupling.shape, F32),
+            pltpu.VMEM((1, STATES), F32),
+            pltpu.VMEM((1, STATES), F32),
+            pltpu.VMEM((1, STATES), F32),
+            pltpu.VMEM((1, FIB), jnp.int32),
+            pltpu.VMEM((1, FIB), jnp.int32),
+            pltpu.VMEM((1, FIB), jnp.int32),
+            pltpu.VMEM((1, stim_step.shape[0]), jnp.int32),
+            pltpu.VMEM(tissue.shape, F32),
+            pltpu.VMEM(local.shape, F32),
+            pltpu.VMEM(far.shape, F32),
             pltpu.VMEM((ROWS, NODES, FIB), F32),
             pltpu.VMEM((NODES, ROWS, FIB), F32),
             pltpu.VMEM((NODES, ROWS, FIB), F32),
@@ -471,7 +511,7 @@
             pltpu.VMEM((BINS, BY, BZ), F32),
             pltpu.VMEM((BINS, BY, BZ), F32),
             pltpu.SemaphoreType.DMA((4,)),
-            pltpu.SemaphoreType.DMA((4,)),
+            pltpu.SemaphoreType.DMA((12,)),
             pltpu.SemaphoreType.DMA((3,)),
             pltpu.SemaphoreType.DMA((3,)),
             pltpu.SemaphoreType.DMA((STEPS,)),
@@ -479,12 +519,20 @@
             pltpu.SemaphoreType.DMA((STEPS, sweeps)),
             pltpu.SemaphoreType.DMA((STEPS, sweeps)),
         ],
-        compiler_params=pltpu.CompilerParams(collective_id=0, has_side_effects=True),
-    )(
+        compiler_params=pltpu.CompilerParams(collective_id=0, has_side_effects=True, vmem_limit_bytes=VMEM_LIMIT),
+    )(*(pltpu.with_memory_space_constraint(array, pltpu.HBM) for array in (
         states, voltage, coupling, decay_rates.reshape(1, -1), volt_gain.reshape(1, -1),
         current_weights.reshape(1, -1), fibre_home.reshape(1, -1), cross_cell.reshape(1, -1),
         motor_unit.reshape(1, -1), stim_step.reshape(1, -1), tissue, local, far,
-    )
+    )))
+    return pl.pallas_call(
+        write_out,
+        out_shape=tuple(jax.ShapeDtypeStruct(array.shape, F32) for array in outputs),
+        in_specs=[vmem] * 3,
+        out_specs=(pl.BlockSpec(memory_space=pl.ANY),) * 3,
+        scratch_shapes=[pltpu.SemaphoreType.DMA((6,))],
+        compiler_params=pltpu.CompilerParams(vmem_limit_bytes=VMEM_LIMIT),
+    )(*(pltpu.with_memory_space_constraint(array, pltpu.VMEM) for array in outputs))
 
 
 def solution(mesh):

time: 49.9 us -> 37.6 us (0.75); the launches traced: 49 us -> 37.5 us
  Pallas kernels: 44 us -> 36.8 us
  local copies, waits for them, and re-layouts: 4.34 us -> 0 us
    pallas_call x1, Pallas kernels: 44 us -> 35.5 us  [on_device(): pl.pallas_call(kernel, out_shape=(jax.ShapeDtypeStruct(states.shape, F32)...]
    unnamed x7 -> x0, local copies, waits for them, and re-layouts: 4.34 us -> none
    pallas_call x0 -> x1, Pallas kernels: none -> 1.37 us  [on_device(): pl.pallas_call(write_out, out_shape=tuple((jax.ShapeDtypeStruct(array.sha...]
where the time goes in v2:
time: 37.6 us; the launch traced here: 37.5 us
  Pallas kernels  36.8 us (98%)
  between operations  0.64 us (2%)
    pallas_call x1, Pallas kernels, on_device(): pl.pallas_call(kernel, out_shape=(jax.ShapeDtypeStruct(states.shape, F32)...  35.5 us
    pallas_call x1, Pallas kernels, on_device(): pl.pallas_call(write_out, out_shape=tuple((jax.ShapeDtypeStruct(array.sha...  1.37 us

profile of v2, /device:TPU:1, one launch (start us, length us, event | category | flops | bytes accessed | tf_op | source)
XLA Modules:
  0.0 37.5 jit_solution(6404938090316808661)
XLA Ops:
  0.6 35.5 %shard_map.148 = (f32[57,64,128]{2,1,0:T(8,128)S(1)}, f32[64,128]{1,0:T(8,128)S(1)}, f32[2,32,8,128]{3,2,1,0:T(8,128)S(1)}) custom-call(f32[57,64,128]{2,1,0:T(8,128)} %states_hbm.1, f32[64,128]{1,0:T(8,128)} %volt_hbm.1, f32[57,57]{1,0:T(8,128)} %coup_hbm.1, f32[1,57]{1,0:T(1,128)} %bitcast.7, f32[1,57]{1,0:T(1,128)} %bitcast.8, f32[1,57]{1,0:T(1,128)} %bitcast.9, ...), custom_call_target="tpu_custom_call" | custom-call | tf_op jit(solution)/shard_map/pallas_call | solution.py:467
  36.1 1.4 %shard_map.149 = (f32[57,64,128]{2,1,0:T(8,128)}, f32[64,128]{1,0:T(8,128)}, f32[2,32,8,128]{3,2,1,0:T(8,128)}) custom-call(f32[57,64,128]{2,1,0:T(8,128)S(1)} %get-tuple-element.6.states, f32[64,128]{1,0:T(8,128)S(1)} %get-tuple-element.7.voltage, f32[2,32,8,128]{3,2,1,0:T(8,128)S(1)} %get-tuple-element.8.potential), custom_call_target="tpu_custom_call" | custom-call | tf_op jit(solution)/shard_map/pallas_call | solution.py:528

commit v3 on v2

--- a/solution.py
+++ b/solution.py
@@ -34,8 +34,11 @@
 BY, BZ = 8, 128
 SLOT_ROWS = 4
 CAPACITY = 12
-FACE_ROWS = 112
+WIDE_ROWS = 304
+Z_TILES = 24
+WRAP = 48
 VMEM_LIMIT = 24 << 20
+UNROLL = 31
 
 
 def cable_tables():
@@ -97,9 +100,10 @@
     volt_ref, coup_ref, decay_ref, gain_ref, wts_ref, home_ref, cell_ref, mu_ref,
     stim_ref, tissue_ref, local_ref, far_ref,
     s_in, s_work, s_new, lhs_ref, keep_ref, gain_b, wts_b, cur_ref, v1_ref, hot_ref, sel_ref,
-    cell_send, cell_recv, row_send, row_recv, end_send, end_recv, face_send, face_recv,
-    d_ref, r_ref, x_ref, hy_ref, hz_ref,
-    in_sem, small_sem, a2a_send, a2a_recv, len_send, len_recv, face_ssem, face_rsem,
+    cell_send, cell_recv, row_send, row_recv, end_send, end_recv,
+    own_ref, x_ref, r_ref, d_ref, t_ref, zr_ref, zd_ref, zt_ref, hz_ref,
+    y_send, z_send, wide_recv, z_recv,
+    in_sem, small_sem, a2a_send, a2a_recv, len_send, len_recv, halo_ssem, halo_rsem,
 ):
     fib, shard, emg = lax.axis_index("fib"), lax.axis_index("len"), lax.axis_index("emg")
     me = fib * N_EMG + emg
@@ -131,6 +135,13 @@
         other = lax.rem(me + step, GROUPS)
         return {"fib": other // N_EMG, "len": shard, "emg": lax.rem(other, N_EMG)}, other
 
+    def towards(df, dl, de):
+        return {
+            "fib": lax.rem(fib + N_FIB + df, N_FIB),
+            "len": lax.rem(shard + N_LEN + dl, N_LEN),
+            "emg": lax.rem(emg + N_EMG + de, N_EMG),
+        }
+
     def greet(step, _):
         device, _other = peer(step)
         pl.semaphore_signal(barrier, inc=1, device_id=device, device_id_type=MESH)
@@ -142,6 +153,14 @@
         pl.semaphore_signal(
             barrier, inc=1, device_id={"fib": fib, "len": other, "emg": emg}, device_id_type=MESH
         )
+
+    for df in (-1, 0, 1):
+        for de in (-1, 0, 1):
+            for dl in (-1, 1):
+                if (df, de) != (0, 0):
+                    pl.semaphore_signal(
+                        barrier, inc=1, device_id=towards(df, dl, de), device_id_type=MESH
+                    )
 
     def column(row):
         wide = row.shape[1]
@@ -205,7 +224,7 @@
             ).start()
             return 0
 
-        lax.fori_loop(1, GROUPS, send, 0)
+        lax.fori_loop(1, GROUPS, send, 0, unroll=UNROLL)
         target[me] = source[me]
 
     def exchange_wait(target, slot_index):
@@ -252,10 +271,8 @@
     for part in range(4):
         loads[part].wait()
         lax.fori_loop(part * (quarter // 2), (part + 1) * (quarter // 2), first_pair, 0, unroll=8)
-        if part == 1:
-            pl.semaphore_wait(barrier, GROUPS - 1 + N_LEN - 1)
-            exchange(cell_send, cell_recv, 0)
-
+
+    pl.semaphore_wait(barrier, GROUPS - 1 + N_LEN - 1 + 16)
     node_id = shard * NODES + iota((NODES, FIB), 0)
     total_nodes = NODES * N_LEN
     band = (node_id >= total_nodes // 2 - band_half) & (node_id < total_nodes // 2 + band_half)
@@ -287,8 +304,231 @@
         return first + second
 
     local = cable_begin(0, volt_ref[...])
+    exchange(cell_send, cell_recv, 0)
     row_send[0] = pack(binned())
     exchange(row_send.at[0], row_recv.at[0], 1)
+
+    middle = 0.5 * (high_bound + low_bound)
+    spread_width = 0.5 * (high_bound - low_bound)
+    ratio = middle / spread_width
+    lane = iota((BY, BZ), 1)
+    sub = iota((BY, BZ), 0)
+    zlane = iota((8, WRAP * BY), 1)
+    zsub = iota((8, WRAP * BY), 0)
+    zrow = lax.rem(zlane, BY)
+
+    def inside(condition):
+        return jnp.where(condition, 1.0, 0.0).astype(F32)
+
+    fib_up, fib_down = inside(fib < N_FIB - 1), inside(fib > 0)
+    len_up, len_down = inside(shard < N_LEN - 1), inside(shard > 0)
+    emg_up, emg_down = inside(emg < N_EMG - 1), inside(emg > 0)
+    margin = jnp.where(sub < 4, fib_up, fib_down)
+    zmask = jnp.where(zsub < 4, emg_up, emg_down)
+    zmask = zmask * jnp.where(zlane < 256, 1.0, jnp.where(zlane < 320, len_up, len_down))
+    zmasks = (zmask, zmask * jnp.where(zrow < 4, fib_up, fib_down))
+
+    def spread_out(kind, own):
+        flat = own.reshape(BINS * BY, BZ)
+        pick = jnp.where(iota((8, BZ), 0) < 4, iota((8, BZ), 0), iota((8, BZ), 0) + BZ - 8)
+        pick = (iota((8, BZ), 1) == pick).astype(F32)
+        side = dot_t(pick, flat[...], HIGH)
+        for half in range(2):
+            for tile in range(2):
+                z_send[kind, half, tile] = side[4 * half :][:4, tile * BZ :][:, :BZ]
+        for y in range(3):
+            y_send[kind, 0, y * BINS : (y + 1) * BINS, :] = flat[pl.ds(y, BINS, stride=BY), :]
+            y_send[kind, 1, y * BINS : (y + 1) * BINS, :] = flat[pl.ds(BY - 3 + y, BINS, stride=BY), :]
+
+        def post(source, target, sem, device):
+            pltpu.make_async_remote_copy(
+                source, target, halo_ssem.at[kind, sem], halo_rsem.at[kind, sem],
+                device_id=device, device_id_type=MESH,
+            ).start()
+
+        wide, tiles = wide_recv.at[kind], z_recv.at[kind]
+        for half, de in ((0, -1), (1, 1)):
+            base = 12 * half
+            for f, df in enumerate((-1, 1)):
+                for x, dl in enumerate((-1, 1)):
+                    post(
+                        z_send.at[kind, half, pl.ds(x, 1)],
+                        tiles.at[pl.ds(base + 8 + 2 * f + x, 1)], 1, towards(df, dl, de),
+                    )
+            for f, df in enumerate((-1, 1)):
+                post(
+                    z_send.at[kind, half], tiles.at[pl.ds(base + 4 + 2 * f, 2)], 1, towards(df, 0, de)
+                )
+            for x, dl in enumerate((-1, 1)):
+                post(
+                    z_send.at[kind, half, pl.ds(x, 1)], tiles.at[pl.ds(base + 2 + x, 1)], 1,
+                    towards(0, dl, de),
+                )
+            post(z_send.at[kind, half], tiles.at[pl.ds(base, 2)], 1, towards(0, 0, de))
+        for f, df in enumerate((-1, 1)):
+            for x, dl in enumerate((-1, 1)):
+                post(
+                    flat.at[pl.ds(x * (BINS - 2) * BY, 2 * BY)],
+                    wide.at[pl.ds(240 + 32 * f + 16 * x, 16)], 0, towards(df, dl, 0),
+                )
+        post(y_send.at[kind, 0], wide.at[pl.ds(96, 96)], 0, towards(-1, 0, 0))
+        post(y_send.at[kind, 1], wide.at[pl.ds(0, 96)], 0, towards(1, 0, 0))
+        post(flat.at[pl.ds(0, 24)], wide.at[pl.ds(216, 24)], 0, towards(0, -1, 0))
+        post(flat.at[pl.ds((BINS - 3) * BY, 24)], wide.at[pl.ds(192, 24)], 0, towards(0, 1, 0))
+
+    def assemble(kind, own, field, zfield, add):
+        def plus(values):
+            return values + add if add else values
+
+        wide, tiles = wide_recv.at[kind], z_recv.at[kind]
+        pltpu.make_async_copy(wide, wide, halo_rsem.at[kind, 0]).wait()
+        pltpu.make_async_copy(tiles, tiles, halo_rsem.at[kind, 1]).wait()
+        field[0, pl.ds(0, BINS)] = plus(own[...])
+        for k in range(3):
+            field[0, BINS + k] = plus(wide[216 + 8 * k : 224 + 8 * k, :] * len_up)
+            field[0, WRAP - 3 + k] = plus(wide[192 + 8 * k : 200 + 8 * k, :] * len_down)
+        beside = field.at[1].reshape(WRAP * BY, BZ)
+        for y in range(3):
+            beside[pl.ds(y, BINS, stride=BY), :] = plus(wide[96 + 32 * y : 128 + 32 * y, :] * fib_up)
+            beside[pl.ds(BY - 3 + y, BINS, stride=BY), :] = plus(wide[32 * y : 32 * y + 32, :] * fib_down)
+        for k in range(2):
+            for x, (place, weight) in enumerate(((BINS, len_up), (WRAP - 2, len_down))):
+                start = 240 + 16 * x + 8 * k
+                up, down = wide[start : start + 8, :], wide[start + 32 : start + 40, :]
+                edge = jnp.where(sub < 4, up * fib_up, down * fib_down)
+                field[1, place + k] = plus(edge * weight)
+        low = iota((4, BZ), 1) < BZ // 2
+        near = lax.rem(iota((4, BZ), 1), BY) < 4
+        for half, weight in ((0, emg_up), (1, emg_down)):
+            base = 12 * half
+            rows = slice(4 * half, 4 * half + 4)
+            for tile in range(2):
+                lanes = slice(tile * BZ, (tile + 1) * BZ)
+                zfield[0, rows, lanes] = plus(tiles[base + tile] * weight)
+                up, down = tiles[base + 4 + tile] * fib_up, tiles[base + 6 + tile] * fib_down
+                zfield[1, rows, lanes] = plus(jnp.where(near, up, down) * weight)
+            lanes = slice(2 * BZ, 3 * BZ)
+            both = jnp.where(low, tiles[base + 2] * len_up, tiles[base + 3] * len_down)
+            zfield[0, rows, lanes] = plus(both * weight)
+            up = jnp.where(low, tiles[base + 8] * len_up, tiles[base + 9] * len_down)
+            down = jnp.where(low, tiles[base + 10] * len_up, tiles[base + 11] * len_down)
+            both = jnp.where(near, up * fib_up, down * fib_down)
+            zfield[1, rows, lanes] = plus(both * weight)
+
+    def scatter(step):
+        exchange_wait(row_recv.at[step], 1 + step)
+        rows = row_recv[step].reshape(packed, FIB)
+        turned = rows.T
+        wide = jnp.concatenate([turned[q * BINS : (q + 1) * BINS] for q in range(4)], axis=1)
+        both = dot(jnp.concatenate(split(wide), axis=0), hot_ref[...])
+        source = both[:BINS] + both[BINS:]
+        flat = own_ref.at[step].reshape(BINS * BY, BZ)
+        for y in range(BY):
+            flat[pl.ds(y, BINS, stride=BY), :] = source[:, y * BZ : (y + 1) * BZ]
+
+    weight = [1.0 / ratio]
+    for _ in range(SWEEPS - 1):
+        weight.append(1.0 / (2.0 * ratio - weight[-1]))
+
+    def sweep(step, turn):
+        first, last = turn == 0, turn == SWEEPS - 2
+        keep = weight[turn + 1] * weight[turn]
+        gain = 2.0 * weight[turn + 1] / spread_width
+        scale = 1.0 / middle if first else 1.0
+        field = r_ref.at[step] if first else d_ref.at[step]
+        zfield = zr_ref.at[step] if first else zd_ref.at[step]
+        inject = ((iota((8, BZ), 0) == BY - 1) & (iota((8, BZ), 1) == 0)).astype(F32)
+        inject = inject + ((iota((8, BZ), 0) == 0) & (iota((8, BZ), 1) == BZ - 1)).astype(F32)
+        ends = ((iota((8, BZ), 0) == 0) & (iota((8, BZ), 1) == BZ - 1)).astype(F32)
+        ends = ends + ((iota((8, BZ), 0) == BY - 1) & (iota((8, BZ), 1) == 0)).astype(F32)
+        count = BINS if last else WRAP
+        for tile in range(1 if last else 2):
+            injected = dot_tl(zfield[tile, :, : count * BY], inject, HIGH)
+            hz_ref[tile, pl.ds(0, count)] = injected.reshape(count, BY, BZ)
+
+        def advance(here, beside, diagonal, rest, push):
+            if first:
+                rest = here - scale * (diagonal * here - beside)
+            else:
+                rest = rest - (diagonal * here - beside)
+            return rest, (keep * scale) * here + push * rest
+
+        if not last:
+            zs = [zfield[0], zfield[1]]
+            edges = [dot_t(ends, field.at[t].reshape(WRAP * BY, BZ)[...], HIGH) for t in range(2)]
+            up = [pltpu.roll(z, 1, 1) for z in zs]
+            down = [pltpu.roll(z, WRAP * BY - 1, 1) for z in zs]
+            up_far = [pltpu.roll(z, WRAP * BY - BY + 1, 1) for z in zs]
+            down_far = [pltpu.roll(z, BY - 1, 1) for z in zs]
+            for t in range(2):
+                beside = pltpu.roll(zs[t], BY, 1) + pltpu.roll(zs[t], WRAP * BY - BY, 1)
+                beside = beside + jnp.where(zrow == 0, up_far[1 - t], up[t])
+                beside = beside + jnp.where(zrow == BY - 1, down_far[1 - t], down[t])
+                beside = beside + jnp.where(zsub == 0, edges[t], pltpu.roll(zs[t], 1, 0))
+                beside = beside + jnp.where(zsub == 7, edges[t], pltpu.roll(zs[t], 7, 0))
+                rest, after = advance(
+                    zs[t], beside, zt_ref[t], None if first else zr_ref[step, t], gain * zmasks[t]
+                )
+                zr_ref[step, t] = rest
+                zd_ref[step, t] = after
+
+        def slab(place, following, previous, push, own):
+            here = (field[0, place], field[1, place])
+            up = [pltpu.roll(h, 1, 0) for h in here]
+            down = [pltpu.roll(h, BY - 1, 0) for h in here]
+            for t in range(1 if last else 2):
+                beside = previous[t] + field[t, following] + hz_ref[t, place]
+                beside = beside + jnp.where(sub == 0, up[1 - t], up[t])
+                beside = beside + jnp.where(sub == BY - 1, down[1 - t], down[t])
+                beside = beside + jnp.where(lane == 0, 0.0, pltpu.roll(here[t], 1, 1))
+                beside = beside + jnp.where(lane == BZ - 1, 0.0, pltpu.roll(here[t], BZ - 1, 1))
+                rest, after = advance(
+                    here[t], beside, t_ref[t, place], None if first else r_ref[step, t, place],
+                    push if t == 0 else push * margin,
+                )
+                if not last:
+                    r_ref[step, t, place] = rest
+                    d_ref[step, t, place] = after
+                if own and t == 0:
+                    if last:
+                        pot_out[step, place] = x_ref[step, place] + after
+                    elif first:
+                        x_ref[step, place] = scale * here[0] + after
+                    else:
+                        x_ref[step, place] = x_ref[step, place] + after
+            return here
+
+        reach = SWEEPS - 2 - turn
+        start = (WRAP - 1 - reach) % WRAP
+        previous = (field[0, start], field[1, start])
+        for k in range(reach):
+            place = start + 1 + k
+            previous = slab(place, (place + 1) % WRAP, previous, gain * len_down, False)
+        previous = lax.fori_loop(
+            0, BINS, lambda x, before: slab(x, x + 1, before, gain, True), previous, unroll=8
+        )
+        for k in range(reach):
+            previous = slab(BINS + k, BINS + k + 1, previous, gain * len_up, False)
+
+    spread_out(STEPS, tissue_ref)
+    r_ref[...] = jnp.zeros_like(r_ref)
+    d_ref[...] = jnp.zeros_like(d_ref)
+    t_ref[...] = jnp.zeros_like(t_ref)
+    v1_ref[...] = cable_end(0, local)
+
+    o_flat = states_out.reshape(STATES * NODES, FIB)
+
+    def second(node, _):
+        drive = s_new[node] + gain_b[...] * v1_ref[pl.ds(node, 1), :]
+        new = keep_ref[...] * s_work[node] + time_step * jnp.tanh(drive)
+        o_flat[pl.ds(node, STATES, stride=NODES), :] = new[:STATES]
+        cur_ref[pl.ds(node, 1), :] = jnp.sum(wts_b[...] * new, axis=0, keepdims=True)
+        return 0
+
+    lax.fori_loop(0, NODES, second, 0, unroll=8)
+    row_send[1] = pack(binned())
+    exchange(row_send.at[1], row_recv.at[1], 2)
+    local = cable_begin(1, v1_ref[...])
 
     exchange_wait(cell_recv, 0)
     cells = cell_recv[...].reshape(packed, FIB)
@@ -298,144 +538,25 @@
             hot = (column_q == iota((packed, BZ), 1) + y * BZ).astype(F32).astype(BF16)
             hot_ref[q * packed : (q + 1) * packed, y * BZ : (y + 1) * BZ] = hot
 
-    middle = 0.5 * (high_bound + low_bound)
-    spread_width = 0.5 * (high_bound - low_bound)
-    ratio = middle / spread_width
-    lane = iota((BY, BZ), 1)
-    sub = iota((BY, BZ), 0)
-
-    def scatter(step):
-        exchange_wait(row_recv.at[step], 1 + step)
-        rows = row_recv[step].reshape(packed, FIB)
-        turned = rows.T
-        wide = jnp.concatenate([turned[q * BINS : (q + 1) * BINS] for q in range(4)], axis=1)
-        both = dot(jnp.concatenate(split(wide), axis=0), hot_ref[...])
-        source = both[:BINS] + both[BINS:]
-        flat = r_ref.at[step].reshape(BINS * BY, BZ)
-        for y in range(BY):
-            flat[pl.ds(y, BINS, stride=BY), :] = source[:, y * BZ : (y + 1) * BZ]
-        first = r_ref[step] * (1.0 / middle)
-        d_ref[step, pl.ds(1, BINS)] = first
-        x_ref[step] = first
-
-    def faces(step, sweep):
-        send = face_send.at[step, sweep]
-        recv = face_recv.at[step, sweep]
-        flat = d_ref.at[step].reshape((BINS + 2) * BY, BZ)
-        send[0:32, :] = flat[pl.ds(BY, BINS, stride=BY), :]
-        send[32:64, :] = flat[pl.ds(2 * BY - 1, BINS, stride=BY), :]
-        send[64:72, :] = flat[BY : 2 * BY, :]
-        send[72:80, :] = flat[BINS * BY : (BINS + 1) * BY, :]
-        pick = (iota((8, BZ), 1) == (BZ - 1) * iota((8, BZ), 0)).astype(F32)
-        side = dot_t(pick, flat[BY : (BINS + 1) * BY, :], HIGH)
-        send[80:88, :] = side[:, :BZ]
-        send[88:96, :] = side[:, BZ:]
-        up, down = lax.rem(fib + 1, N_FIB), lax.rem(fib + N_FIB - 1, N_FIB)
-        right, left = lax.rem(shard + 1, N_LEN), lax.rem(shard + N_LEN - 1, N_LEN)
-        front, back = lax.rem(emg + 1, N_EMG), lax.rem(emg + N_EMG - 1, N_EMG)
-        plan = (
-            (0, 32, 32, {"fib": down, "len": shard, "emg": emg}),
-            (32, 0, 32, {"fib": up, "len": shard, "emg": emg}),
-            (64, 72, 8, {"fib": fib, "len": left, "emg": emg}),
-            (72, 64, 8, {"fib": fib, "len": right, "emg": emg}),
-            (80, 96, 16, {"fib": fib, "len": shard, "emg": back}),
-            (80, 80, 16, {"fib": fib, "len": shard, "emg": front}),
-        )
-        for source, target, height, device in plan:
-            pltpu.make_async_remote_copy(
-                send.at[pl.ds(source, height)], recv.at[pl.ds(target, height)],
-                face_ssem.at[step, sweep], face_rsem.at[step, sweep],
-                device_id=device, device_id_type=MESH,
-            ).start()
-
-    def sweep_on(step, sweep, weight_now, weight_next):
-        recv = face_recv.at[step, sweep]
-        pltpu.make_async_copy(recv, recv, face_rsem.at[step, sweep]).wait()
-
-        def unless(edge):
-            return jnp.where(edge, 0.0, 1.0).astype(F32)
-
-        d_ref[step, 0] = recv[64:72, :] * unless(shard == 0)
-        d_ref[step, BINS + 1] = recv[72:80, :] * unless(shard == N_LEN - 1)
-        hy_flat = hy_ref.reshape(BINS * BY, BZ)
-        hy_flat[pl.ds(0, BINS, stride=BY), :] = recv[0:32, :] * unless(fib == 0)
-        hy_flat[pl.ds(BY - 1, BINS, stride=BY), :] = recv[32:64, :] * unless(fib == N_FIB - 1)
-        low_side = jnp.concatenate([recv[80:88, :], recv[88:96, :]], axis=1)
-        high_side = jnp.concatenate([recv[96:104, :], recv[104:112, :]], axis=1)
-        row, col = iota((16, BZ), 0), iota((16, BZ), 1)
-        inject = jnp.where((row == 1) & (col == 0), unless(emg == 0), 0.0)
-        inject = inject + jnp.where((row == 8) & (col == BZ - 1), unless(emg == N_EMG - 1), 0.0)
-        hz_ref[...] = dot_tl(jnp.concatenate([low_side, high_side], axis=0), inject, HIGH).reshape(
-            BINS, BY, BZ
-        )
-        keep, gain = weight_next * weight_now, 2.0 * weight_next / spread_width
-
-        def slab(x, previous):
-            here = d_ref[step, x + 1]
-            beside = previous + d_ref[step, x + 2] + hy_ref[x] + hz_ref[x]
-            beside = beside + jnp.where(sub == 0, 0.0, pltpu.roll(here, 1, 0))
-            beside = beside + jnp.where(sub == BY - 1, 0.0, pltpu.roll(here, BY - 1, 0))
-            beside = beside + jnp.where(lane == 0, 0.0, pltpu.roll(here, 1, 1))
-            beside = beside + jnp.where(lane == BZ - 1, 0.0, pltpu.roll(here, BZ - 1, 1))
-            rest = r_ref[step, x] - ((6.0 + tissue_ref[x]) * here - beside)
-            after = keep * here + gain * rest
-            r_ref[step, x] = rest
-            d_ref[step, x + 1] = after
-            if sweep == SWEEPS - 2:
-                pot_out[step, x] = x_ref[step, x] + after
-            else:
-                x_ref[step, x] = x_ref[step, x] + after
-            return here
-
-        lax.fori_loop(0, BINS, slab, d_ref[step, 0], unroll=16)
-
-    weight = [1.0 / ratio]
-    for _ in range(SWEEPS - 1):
-        weight.append(1.0 / (2.0 * ratio - weight[-1]))
-
-    def advance(step, sweep):
-        sweep_on(step, sweep, weight[sweep], weight[sweep + 1])
-        if sweep < SWEEPS - 2:
-            faces(step, sweep + 1)
-
-    v1_ref[...] = cable_end(0, local)
-
-    o_flat = states_out.reshape(STATES * NODES, FIB)
-
-    def second(node, _):
-        drive = s_new[node] + gain_b[...] * v1_ref[pl.ds(node, 1), :]
-        new = keep_ref[...] * s_work[node] + time_step * jnp.tanh(drive)
-        o_flat[pl.ds(node, STATES, stride=NODES), :] = new[:STATES]
-        cur_ref[pl.ds(node, 1), :] = jnp.sum(wts_b[...] * new, axis=0, keepdims=True)
-        return 0
-
-    lax.fori_loop(0, NODES // 2, second, 0, unroll=8)
     scatter(0)
-    faces(0, 0)
-    lax.fori_loop(NODES // 2, NODES, second, 0, unroll=8)
-
-    row_send[1] = pack(binned())
-    exchange(row_send.at[1], row_recv.at[1], 2)
-    local = cable_begin(1, v1_ref[...])
-
-    advance(0, 0)
+    spread_out(0, own_ref.at[0])
+    assemble(STEPS, tissue_ref, t_ref, zt_ref, 6.0)
     volt_out[...] = cable_end(1, local)
     scatter(1)
-    faces(1, 0)
-    advance(0, 1)
-    advance(1, 0)
-    advance(0, 2)
-    advance(1, 1)
-    advance(1, 2)
+    spread_out(1, own_ref.at[1])
+    for step in range(STEPS):
+        assemble(step, own_ref.at[step], r_ref.at[step], zr_ref.at[step], 0.0)
+        for turn in range(SWEEPS - 1):
+            sweep(step, turn)
 
     exchange_sent(cell_send, 0)
     for step in range(STEPS):
         exchange_sent(row_send.at[step], 1 + step)
         whole = end_recv.at[step, pl.ds(0, N_LEN - 1)]
         pltpu.make_async_copy(whole, whole, len_send.at[step]).wait()
-        for sweep in range(SWEEPS - 1):
-            sent = face_send.at[step, sweep]
-            pltpu.make_async_copy(sent, sent, face_ssem.at[step, sweep]).wait()
+    for kind in range(STEPS + 1):
+        for number, sent in enumerate((wide_recv.at[kind], z_recv.at[kind])):
+            pltpu.make_async_copy(sent, sent, halo_ssem.at[kind, number]).wait()
 
 
 def write_out(states, voltage, potential, states_out, voltage_out, potential_out, sem):
@@ -463,7 +584,6 @@
     local, far = cable_tables()
     vmem = pl.BlockSpec(memory_space=pltpu.VMEM)
     hbm = pl.BlockSpec(memory_space=pltpu.HBM)
-    sweeps = SWEEPS - 1
     outputs = pl.pallas_call(
         kernel,
         out_shape=(
@@ -503,21 +623,27 @@
             pltpu.VMEM((STEPS, GROUPS, SLOT_ROWS, FIB), F32),
             pltpu.VMEM((STEPS, 8, FIB), F32),
             pltpu.VMEM((STEPS, N_LEN, 8, FIB), F32),
-            pltpu.VMEM((STEPS, sweeps, FACE_ROWS, FIB), F32),
-            pltpu.VMEM((STEPS, sweeps, FACE_ROWS, FIB), F32),
-            pltpu.VMEM((STEPS, BINS + 2, BY, BZ), F32),
             pltpu.VMEM((STEPS, BINS, BY, BZ), F32),
             pltpu.VMEM((STEPS, BINS, BY, BZ), F32),
-            pltpu.VMEM((BINS, BY, BZ), F32),
-            pltpu.VMEM((BINS, BY, BZ), F32),
+            pltpu.VMEM((STEPS, 2, WRAP, BY, BZ), F32),
+            pltpu.VMEM((STEPS, 2, WRAP, BY, BZ), F32),
+            pltpu.VMEM((2, WRAP, BY, BZ), F32),
+            pltpu.VMEM((STEPS, 2, 8, WRAP * BY), F32),
+            pltpu.VMEM((STEPS, 2, 8, WRAP * BY), F32),
+            pltpu.VMEM((2, 8, WRAP * BY), F32),
+            pltpu.VMEM((2, WRAP, BY, BZ), F32),
+            pltpu.VMEM((STEPS + 1, 2, 3 * BINS, BZ), F32),
+            pltpu.VMEM((STEPS + 1, 2, 2, 4, BZ), F32),
+            pltpu.VMEM((STEPS + 1, WIDE_ROWS, BZ), F32),
+            pltpu.VMEM((STEPS + 1, Z_TILES, 4, BZ), F32),
             pltpu.SemaphoreType.DMA((4,)),
             pltpu.SemaphoreType.DMA((12,)),
             pltpu.SemaphoreType.DMA((3,)),
             pltpu.SemaphoreType.DMA((3,)),
             pltpu.SemaphoreType.DMA((STEPS,)),
             pltpu.SemaphoreType.DMA((STEPS,)),
-            pltpu.SemaphoreType.DMA((STEPS, sweeps)),
-            pltpu.SemaphoreType.DMA((STEPS, sweeps)),
+            pltpu.SemaphoreType.DMA((STEPS + 1, 2)),
+            pltpu.SemaphoreType.DMA((STEPS + 1, 2)),
         ],
         compiler_params=pltpu.CompilerParams(collective_id=0, has_side_effects=True, vmem_limit_bytes=VMEM_LIMIT),
     )(*(pltpu.with_memory_space_constraint(array, pltpu.HBM) for array in (

time: 37.6 us -> 32.5 us (0.86)
  Pallas kernels: 36.8 us -> 31.7 us
    pallas_call x1, Pallas kernels: 35.5 us -> 30.3 us  [on_device(): pl.pallas_call(kernel, out_shape=(jax.ShapeDtypeStruct(states.shape, F32)...]
where the time goes in v3:
time: 32.5 us; the launch traced here: 32.4 us
  Pallas kernels  31.7 us (98%)
  between operations  0.64 us (2%)
    pallas_call x1, Pallas kernels, on_device(): pl.pallas_call(kernel, out_shape=(jax.ShapeDtypeStruct(states.shape, F32)...  30.3 us
    pallas_call x1, Pallas kernels, on_device(): pl.pallas_call(write_out, out_shape=tuple((jax.ShapeDtypeStruct(array.sha...  1.37 us

profile of v3, /device:TPU:1, one launch (start us, length us, event | category | flops | bytes accessed | tf_op | source)
XLA Modules:
  0.0 32.4 jit_solution(2547846349651851549)
XLA Ops:
  0.6 30.3 %shard_map.148 = (f32[57,64,128]{2,1,0:T(8,128)S(1)}, f32[64,128]{1,0:T(8,128)S(1)}, f32[2,32,8,128]{3,2,1,0:T(8,128)S(1)}) custom-call(f32[57,64,128]{2,1,0:T(8,128)} %states_hbm.1, f32[64,128]{1,0:T(8,128)} %volt_hbm.1, f32[57,57]{1,0:T(8,128)} %coup_hbm.1, f32[1,57]{1,0:T(1,128)} %bitcast.7, f32[1,57]{1,0:T(1,128)} %bitcast.8, f32[1,57]{1,0:T(1,128)} %bitcast.9, ...), custom_call_target="tpu_custom_call" | custom-call | tf_op jit(solution)/shard_map/pallas_call | solution.py:587
  31.0 1.4 %shard_map.149 = (f32[57,64,128]{2,1,0:T(8,128)}, f32[64,128]{1,0:T(8,128)}, f32[2,32,8,128]{3,2,1,0:T(8,128)}) custom-call(f32[57,64,128]{2,1,0:T(8,128)S(1)} %get-tuple-element.6.states, f32[64,128]{1,0:T(8,128)S(1)} %get-tuple-element.7.voltage, f32[2,32,8,128]{3,2,1,0:T(8,128)S(1)} %get-tuple-element.8.potential), custom_call_target="tpu_custom_call" | custom-call | tf_op jit(solution)/shard_map/pallas_call | solution.py:654

commit v4 on v3

--- a/solution.py
+++ b/solution.py
@@ -39,6 +39,7 @@
 WRAP = 48
 VMEM_LIMIT = 24 << 20
 UNROLL = 31
+WRITES = 12
 
 
 def cable_tables():
@@ -103,12 +104,11 @@
     cell_send, cell_recv, row_send, row_recv, end_send, end_recv,
     own_ref, x_ref, r_ref, d_ref, t_ref, zr_ref, zd_ref, zt_ref, hz_ref,
     y_send, z_send, wide_recv, z_recv,
-    in_sem, small_sem, a2a_send, a2a_recv, len_send, len_recv, halo_ssem, halo_rsem,
+    in_sem, out_sem, small_sem, a2a_send, a2a_recv, len_send, len_recv, halo_ssem, halo_rsem,
 ):
     fib, shard, emg = lax.axis_index("fib"), lax.axis_index("len"), lax.axis_index("emg")
     me = fib * N_EMG + emg
 
-    quarter = NODES // 4
     smalls = [
         pltpu.make_async_copy(source, target, small_sem.at[number])
         for number, (source, target) in enumerate((
@@ -118,17 +118,8 @@
             (tissue_hbm, tissue_ref),
         ))
     ]
-    for copy in smalls:
+    for copy in smalls[:4] + smalls[8:9]:
         copy.start()
-    loads = []
-    for part in range(4):
-        window = pl.ds(part * quarter, quarter)
-        copy = pltpu.make_async_copy(
-            states_hbm.at[:, window, :], s_in.at[pl.ds(0, STATES), window, :], in_sem.at[part]
-        )
-        copy.start()
-        loads.append(copy)
-
     barrier = pltpu.get_barrier_semaphore()
 
     def peer(step):
@@ -147,7 +138,7 @@
         pl.semaphore_signal(barrier, inc=1, device_id=device, device_id_type=MESH)
         return 0
 
-    lax.fori_loop(1, GROUPS, greet, 0)
+    lax.fori_loop(1, GROUPS, greet, 0, unroll=UNROLL)
     for step in range(1, N_LEN):
         other = lax.rem(shard + step, N_LEN)
         pl.semaphore_signal(
@@ -162,12 +153,26 @@
                         barrier, inc=1, device_id=towards(df, dl, de), device_id_type=MESH
                     )
 
+    s_in[:, pl.ds(STATES, ROWS - STATES), :] = jnp.zeros((NODES, ROWS - STATES, FIB), F32)
+    quarter = NODES // 4
+    for part in range(4):
+
+        def take(node, _, part=part):
+            pltpu.make_async_copy(
+                states_hbm.at[:, node, :], s_in.at[node, pl.ds(0, STATES), :], in_sem.at[part]
+            ).start()
+            return 0
+
+        lax.fori_loop(part * quarter, (part + 1) * quarter, take, 0, unroll=16)
+    for copy in smalls[4:8] + smalls[9:]:
+        copy.start()
+
     def column(row):
         wide = row.shape[1]
         picked = jnp.where(iota((ROWS, wide), 0) == iota((ROWS, wide), 1), row, 0.0)
         return dot_high(picked, jnp.ones((wide, FIB), F32))
 
-    for copy in smalls[:8]:
+    for copy in smalls[:4]:
         copy.wait()
     keep_ref[...] = 1.0 - time_step * column(decay_ref[...])
     gain_b[...] = column(gain_ref[...])
@@ -175,17 +180,85 @@
     spread = (iota((STATES, 3 * ROWS), 0) == lax.rem(iota((STATES, 3 * ROWS), 1), ROWS)).astype(F32)
     tiled = dot_high(coup_ref[...], spread)
     tiled = jnp.concatenate([tiled, jnp.zeros((ROWS - STATES, 3 * ROWS), F32)], axis=0)
-    weights = dot_high(wts_ref[...], spread)
-    tiled = jnp.where(iota((ROWS, 3 * ROWS), 0) == STATES, weights, tiled)
     high, low = split(tiled)
     lhs_ref[...] = jnp.where(iota((ROWS, 3 * ROWS), 1) < 2 * ROWS, high.astype(F32), low.astype(F32)).astype(BF16)
 
+
+    def stacked(values):
+        high, low = split(values)
+        return jnp.concatenate([high, low, high], axis=0)
+
+    def twice(values):
+        return jnp.concatenate([values, values], axis=1)
+
+    def first_pair(pair, _):
+        node = 2 * pair
+        old = jnp.concatenate([s_in[node], s_in[node + 1]], axis=1)
+        volts = jnp.concatenate([volt_ref[pl.ds(node + k, 1), :] for k in range(2)], axis=1)
+        gain = twice(gain_b[...])
+        drive = dot(lhs_ref[...], stacked(old)) + gain * volts
+        new = twice(keep_ref[...]) * old + time_step * jnp.tanh(drive)
+        for k in range(2):
+            part = new[:, k * FIB : (k + 1) * FIB]
+            s_work[node + k] = part
+            cur_ref[pl.ds(node + k, 1), :] = jnp.sum(wts_b[...] * part, axis=0, keepdims=True)
+        return 0
+
+    def next_pair(pair, _):
+        node = 2 * pair
+        new = jnp.concatenate([s_work[node], s_work[node + 1]], axis=1)
+        after = dot(lhs_ref[...], stacked(new))
+        for k in range(2):
+            s_new[node + k] = after[:, k * FIB : (k + 1) * FIB]
+        return 0
+
+    smalls[8].wait()
+
+    for part in range(4):
+        block = s_in.at[pl.ds(part * quarter, quarter), pl.ds(0, STATES), :]
+        pltpu.make_async_copy(block, block, in_sem.at[part]).wait()
+        lax.fori_loop(part * (quarter // 2), (part + 1) * (quarter // 2), first_pair, 0, unroll=8)
+
+    for copy in smalls[4:8] + smalls[9:]:
+        copy.wait()
     unit_hot = (iota((FIB, FIB), 0) == mu_ref[...]).astype(F32)
     stim_row = jnp.concatenate(
         [stim_ref[...].astype(F32), jnp.zeros((1, FIB - stim_ref.shape[1]), F32)], axis=1
     )
     fire = dot(stim_row.astype(BF16), unit_hot.astype(BF16))
 
+    pl.semaphore_wait(barrier, GROUPS - 1 + N_LEN - 1 + 16)
+    node_id = shard * NODES + iota((NODES, FIB), 0)
+    total_nodes = NODES * N_LEN
+    band = (node_id >= total_nodes // 2 - band_half) & (node_id < total_nodes // 2 + band_half)
+
+    def cable_begin(step, volts):
+        active = (fire == float(step)).astype(F32)
+        pulse = jnp.where(band, amplitude * active, 0.0)
+        right = volts + time_step * (pulse - cur_ref[...])
+        both = dot_high(local_ref[shard], right)
+        end_send[step] = both[NODES:]
+        for other_step in range(1, N_LEN):
+            other = lax.rem(shard + other_step, N_LEN)
+            pltpu.make_async_remote_copy(
+                end_send.at[step], end_recv.at[step, shard], len_send.at[step], len_recv.at[step],
+                device_id={"fib": fib, "len": other, "emg": emg}, device_id_type=MESH,
+            ).start()
+        end_recv[step, shard] = jnp.zeros((8, FIB), F32)
+        return both[:NODES]
+
+    def cable_end(step, local):
+        whole = end_recv.at[step, pl.ds(0, N_LEN - 1)]
+        pltpu.make_async_copy(whole, whole, len_recv.at[step]).wait()
+        far = end_recv[step].reshape(8 * N_LEN, FIB)
+        return local + dot_high(far_ref[shard], far)
+
+    def binned():
+        first = cur_ref[pl.ds(0, BINS, stride=2), :]
+        second = cur_ref[pl.ds(1, BINS, stride=2), :]
+        return first + second
+
+    local = cable_begin(0, volt_ref[...])
     home = home_ref[...]
     member = (iota((GROUPS, FIB), 0) == home).astype(F32)
     before = (iota((FIB, FIB), 0) < iota((FIB, FIB), 1)).astype(BF16)
@@ -238,72 +311,6 @@
     cell_row = jnp.broadcast_to(cell_ref[...].astype(F32), (BINS, FIB))
     cell_send[...] = pack(cell_row)
 
-    for copy in smalls[8:]:
-        copy.wait()
-
-    s_flat = s_in.reshape(ROWS * NODES, FIB)
-    s_in[pl.ds(STATES, ROWS - STATES)] = jnp.zeros((ROWS - STATES, NODES, FIB), F32)
-
-    def stacked(values):
-        high, low = split(values)
-        return jnp.concatenate([high, low, high], axis=0)
-
-    def twice(values):
-        return jnp.concatenate([values, values], axis=1)
-
-    def first_pair(pair, _):
-        node = 2 * pair
-        old = jnp.concatenate(
-            [s_flat[pl.ds(node + k, ROWS, stride=NODES), :] for k in range(2)], axis=1
-        )
-        volts = jnp.concatenate([volt_ref[pl.ds(node + k, 1), :] for k in range(2)], axis=1)
-        gain = twice(gain_b[...])
-        drive = dot(lhs_ref[...], stacked(old)) + gain * volts
-        new = twice(keep_ref[...]) * old + time_step * jnp.tanh(drive)
-        after = dot(lhs_ref[...], stacked(new))
-        for k in range(2):
-            lanes = slice(k * FIB, (k + 1) * FIB)
-            s_work[node + k] = new[:, lanes]
-            s_new[node + k] = after[:, lanes]
-            cur_ref[pl.ds(node + k, 1), :] = after[STATES : STATES + 1, lanes]
-        return 0
-
-    for part in range(4):
-        loads[part].wait()
-        lax.fori_loop(part * (quarter // 2), (part + 1) * (quarter // 2), first_pair, 0, unroll=8)
-
-    pl.semaphore_wait(barrier, GROUPS - 1 + N_LEN - 1 + 16)
-    node_id = shard * NODES + iota((NODES, FIB), 0)
-    total_nodes = NODES * N_LEN
-    band = (node_id >= total_nodes // 2 - band_half) & (node_id < total_nodes // 2 + band_half)
-
-    def cable_begin(step, volts):
-        active = (fire == float(step)).astype(F32)
-        pulse = jnp.where(band, amplitude * active, 0.0)
-        right = volts + time_step * (pulse - cur_ref[...])
-        both = dot_high(local_ref[shard], right)
-        end_send[step] = both[NODES:]
-        for other_step in range(1, N_LEN):
-            other = lax.rem(shard + other_step, N_LEN)
-            pltpu.make_async_remote_copy(
-                end_send.at[step], end_recv.at[step, shard], len_send.at[step], len_recv.at[step],
-                device_id={"fib": fib, "len": other, "emg": emg}, device_id_type=MESH,
-            ).start()
-        end_recv[step, shard] = jnp.zeros((8, FIB), F32)
-        return both[:NODES]
-
-    def cable_end(step, local):
-        whole = end_recv.at[step, pl.ds(0, N_LEN - 1)]
-        pltpu.make_async_copy(whole, whole, len_recv.at[step]).wait()
-        far = end_recv[step].reshape(8 * N_LEN, FIB)
-        return local + dot_high(far_ref[shard], far)
-
-    def binned():
-        first = cur_ref[pl.ds(0, BINS, stride=2), :]
-        second = cur_ref[pl.ds(1, BINS, stride=2), :]
-        return first + second
-
-    local = cable_begin(0, volt_ref[...])
     exchange(cell_send, cell_recv, 0)
     row_send[0] = pack(binned())
     exchange(row_send.at[0], row_recv.at[0], 1)
@@ -330,12 +337,10 @@
 
     def spread_out(kind, own):
         flat = own.reshape(BINS * BY, BZ)
-        pick = jnp.where(iota((8, BZ), 0) < 4, iota((8, BZ), 0), iota((8, BZ), 0) + BZ - 8)
-        pick = (iota((8, BZ), 1) == pick).astype(F32)
-        side = dot_t(pick, flat[...], HIGH)
-        for half in range(2):
-            for tile in range(2):
-                z_send[kind, half, tile] = side[4 * half :][:4, tile * BZ :][:, :BZ]
+        for tile in range(2):
+            turned = flat[tile * BZ : (tile + 1) * BZ, :].T
+            z_send[kind, 0, tile] = turned[:4]
+            z_send[kind, 1, tile] = turned[BZ - 4 :]
         for y in range(3):
             y_send[kind, 0, y * BINS : (y + 1) * BINS, :] = flat[pl.ds(y, BINS, stride=BY), :]
             y_send[kind, 1, y * BINS : (y + 1) * BINS, :] = flat[pl.ds(BY - 3 + y, BINS, stride=BY), :]
@@ -437,14 +442,14 @@
         scale = 1.0 / middle if first else 1.0
         field = r_ref.at[step] if first else d_ref.at[step]
         zfield = zr_ref.at[step] if first else zd_ref.at[step]
-        inject = ((iota((8, BZ), 0) == BY - 1) & (iota((8, BZ), 1) == 0)).astype(F32)
-        inject = inject + ((iota((8, BZ), 0) == 0) & (iota((8, BZ), 1) == BZ - 1)).astype(F32)
-        ends = ((iota((8, BZ), 0) == 0) & (iota((8, BZ), 1) == BZ - 1)).astype(F32)
-        ends = ends + ((iota((8, BZ), 0) == BY - 1) & (iota((8, BZ), 1) == 0)).astype(F32)
-        count = BINS if last else WRAP
+        blank = jnp.zeros((BZ - 16, BZ), F32)
         for tile in range(1 if last else 2):
-            injected = dot_tl(zfield[tile, :, : count * BY], inject, HIGH)
-            hz_ref[tile, pl.ds(0, count)] = injected.reshape(count, BY, BZ)
+            for block in range(2 if last else 3):
+                z = zfield[tile, :, block * BZ : (block + 1) * BZ]
+                first_lane = jnp.where(sub == 0, pltpu.roll(z, 1, 0), 0.0)
+                last_lane = jnp.where(sub == 7, pltpu.roll(z, 7, 0), 0.0)
+                turned = jnp.concatenate([first_lane, blank, last_lane], axis=0).T
+                hz_ref[tile, pl.ds(16 * block, 16)] = turned.reshape(16, BY, BZ)
 
         def advance(here, beside, diagonal, rest, push):
             if first:
@@ -455,7 +460,16 @@
 
         if not last:
             zs = [zfield[0], zfield[1]]
-            edges = [dot_t(ends, field.at[t].reshape(WRAP * BY, BZ)[...], HIGH) for t in range(2)]
+            edges = []
+            for t in range(2):
+                parts = []
+                for block in range(3):
+                    turned = field[t, pl.ds(16 * block, 16)].reshape(BZ, BZ).T
+                    ends = jnp.where(
+                        sub == 0, pltpu.roll(turned[BZ - 8 :], 1, 0), pltpu.roll(turned[:8], 7, 0)
+                    )
+                    parts.append(ends)
+                edges.append(jnp.concatenate(parts, axis=1))
             up = [pltpu.roll(z, 1, 1) for z in zs]
             down = [pltpu.roll(z, WRAP * BY - 1, 1) for z in zs]
             up_far = [pltpu.roll(z, WRAP * BY - BY + 1, 1) for z in zs]
@@ -505,7 +519,7 @@
             place = start + 1 + k
             previous = slab(place, (place + 1) % WRAP, previous, gain * len_down, False)
         previous = lax.fori_loop(
-            0, BINS, lambda x, before: slab(x, x + 1, before, gain, True), previous, unroll=8
+            0, BINS, lambda x, before: slab(x, x + 1, before, gain, True), previous, unroll=32
         )
         for k in range(reach):
             previous = slab(BINS + k, BINS + k + 1, previous, gain * len_up, False)
@@ -514,14 +528,13 @@
     r_ref[...] = jnp.zeros_like(r_ref)
     d_ref[...] = jnp.zeros_like(d_ref)
     t_ref[...] = jnp.zeros_like(t_ref)
+    lax.fori_loop(0, NODES // 2, next_pair, 0, unroll=8)
     v1_ref[...] = cable_end(0, local)
-
-    o_flat = states_out.reshape(STATES * NODES, FIB)
 
     def second(node, _):
         drive = s_new[node] + gain_b[...] * v1_ref[pl.ds(node, 1), :]
         new = keep_ref[...] * s_work[node] + time_step * jnp.tanh(drive)
-        o_flat[pl.ds(node, STATES, stride=NODES), :] = new[:STATES]
+        s_in[node] = new
         cur_ref[pl.ds(node, 1), :] = jnp.sum(wts_b[...] * new, axis=0, keepdims=True)
         return 0
 
@@ -540,6 +553,13 @@
 
     scatter(0)
     spread_out(0, own_ref.at[0])
+    def put(node, _):
+        pltpu.make_async_copy(
+            s_in.at[node, pl.ds(0, STATES), :], states_out.at[:, node, :], out_sem.at[0]
+        ).start()
+        return 0
+
+    lax.fori_loop(0, NODES, put, 0, unroll=16)
     assemble(STEPS, tissue_ref, t_ref, zt_ref, 6.0)
     volt_out[...] = cable_end(1, local)
     scatter(1)
@@ -549,6 +569,7 @@
         for turn in range(SWEEPS - 1):
             sweep(step, turn)
 
+    pltpu.make_async_copy(states_out, states_out, out_sem.at[0]).wait()
     exchange_sent(cell_send, 0)
     for step in range(STEPS):
         exchange_sent(row_send.at[step], 1 + step)
@@ -560,17 +581,17 @@
 
 
 def write_out(states, voltage, potential, states_out, voltage_out, potential_out, sem):
-    cuts = (0, 15, 29, 43, STATES)
+    cuts = [STATES * k // WRITES for k in range(WRITES + 1)]
     copies = [
         pltpu.make_async_copy(
             states.at[pl.ds(cuts[k], cuts[k + 1] - cuts[k])],
             states_out.at[pl.ds(cuts[k], cuts[k + 1] - cuts[k])],
             sem.at[k],
         )
-        for k in range(4)
+        for k in range(WRITES)
     ]
-    copies.append(pltpu.make_async_copy(potential, potential_out, sem.at[4]))
-    copies.append(pltpu.make_async_copy(voltage, voltage_out, sem.at[5]))
+    copies.append(pltpu.make_async_copy(potential, potential_out, sem.at[WRITES]))
+    copies.append(pltpu.make_async_copy(voltage, voltage_out, sem.at[WRITES + 1]))
     for copy in copies:
         copy.start()
     for copy in copies:
@@ -606,7 +627,7 @@
             pltpu.VMEM(tissue.shape, F32),
             pltpu.VMEM(local.shape, F32),
             pltpu.VMEM(far.shape, F32),
-            pltpu.VMEM((ROWS, NODES, FIB), F32),
+            pltpu.VMEM((NODES, ROWS, FIB), F32),
             pltpu.VMEM((NODES, ROWS, FIB), F32),
             pltpu.VMEM((NODES, ROWS, FIB), F32),
             pltpu.VMEM((ROWS, 3 * ROWS), BF16),
@@ -637,6 +658,7 @@
             pltpu.VMEM((STEPS + 1, WIDE_ROWS, BZ), F32),
             pltpu.VMEM((STEPS + 1, Z_TILES, 4, BZ), F32),
             pltpu.SemaphoreType.DMA((4,)),
+            pltpu.SemaphoreType.DMA((1,)),
             pltpu.SemaphoreType.DMA((12,)),
             pltpu.SemaphoreType.DMA((3,)),
             pltpu.SemaphoreType.DMA((3,)),
@@ -656,7 +678,7 @@
         out_shape=tuple(jax.ShapeDtypeStruct(array.shape, F32) for array in outputs),
         in_specs=[vmem] * 3,
         out_specs=(pl.BlockSpec(memory_space=pl.ANY),) * 3,
-        scratch_shapes=[pltpu.SemaphoreType.DMA((6,))],
+        scratch_shapes=[pltpu.SemaphoreType.DMA((WRITES + 2,))],
         compiler_params=pltpu.CompilerParams(vmem_limit_bytes=VMEM_LIMIT),
     )(*(pltpu.with_memory_space_constraint(array, pltpu.VMEM) for array in outputs))
 

time: 32.5 us -> 27.3 us (0.84)
  Pallas kernels: 31.7 us -> 26.5 us
    pallas_call x1, Pallas kernels: 30.3 us -> 25 us  [on_device(): pl.pallas_call(kernel, out_shape=(jax.ShapeDtypeStruct(states.shape, F32)...]
where the time goes in v4:
time: 27.3 us; the launch traced here: 27.1 us
  Pallas kernels  26.5 us (97%)
  between operations  0.64 us (2%)
    pallas_call x1, Pallas kernels, on_device(): pl.pallas_call(kernel, out_shape=(jax.ShapeDtypeStruct(states.shape, F32)...  25 us
    pallas_call x1, Pallas kernels, on_device(): pl.pallas_call(write_out, out_shape=tuple((jax.ShapeDtypeStruct(array.sha...  1.44 us

profile of v4, /device:TPU:1, one launch (start us, length us, event | category | flops | bytes accessed | tf_op | source)
XLA Modules:
  0.0 27.1 jit_solution(7177440894127132529)
XLA Ops:
  0.6 25.0 %shard_map.148 = (f32[57,64,128]{2,1,0:T(8,128)S(1)}, f32[64,128]{1,0:T(8,128)S(1)}, f32[2,32,8,128]{3,2,1,0:T(8,128)S(1)}) custom-call(f32[57,64,128]{2,1,0:T(8,128)} %states_hbm.1, f32[64,128]{1,0:T(8,128)} %volt_hbm.1, f32[57,57]{1,0:T(8,128)} %coup_hbm.1, f32[1,57]{1,0:T(1,128)} %bitcast.7, f32[1,57]{1,0:T(1,128)} %bitcast.8, f32[1,57]{1,0:T(1,128)} %bitcast.9, ...), custom_call_target="tpu_custom_call" | custom-call | tf_op jit(solution)/shard_map/pallas_call | solution.py:608
  25.7 1.4 %shard_map.149 = (f32[57,64,128]{2,1,0:T(8,128)}, f32[64,128]{1,0:T(8,128)}, f32[2,32,8,128]{3,2,1,0:T(8,128)}) custom-call(f32[57,64,128]{2,1,0:T(8,128)S(1)} %get-tuple-element.6.states, f32[64,128]{1,0:T(8,128)S(1)} %get-tuple-element.7.voltage, f32[2,32,8,128]{3,2,1,0:T(8,128)S(1)} %get-tuple-element.8.potential), custom_call_target="tpu_custom_call" | custom-call | tf_op jit(solution)/shard_map/pallas_call | solution.py:676

commit v5 on v4

--- a/solution.py
+++ b/solution.py
@@ -1,3 +1,4 @@
+import itertools
 import math
 
 import jax
@@ -34,12 +35,36 @@
 BY, BZ = 8, 128
 SLOT_ROWS = 4
 CAPACITY = 12
-WIDE_ROWS = 304
-Z_TILES = 24
+WIDE_ROWS = 240
+TILES = 28
 WRAP = 48
 VMEM_LIMIT = 24 << 20
-UNROLL = 31
-WRITES = 12
+WRITES = 4
+
+
+def hops(df, dl, de):
+    rows = df % N_FIB
+    return min(rows, N_FIB - rows) / 2 + min(dl % N_LEN, -dl % N_LEN) + min(de % N_EMG, -de % N_EMG)
+
+
+WAYS = [(df, dl, de) for df in (-1, 0, 1) for dl in (-1, 0, 1) for de in (-1, 0, 1)]
+WAYS = sorted((way for way in WAYS if any(way)), key=lambda way: -sum(map(abs, way)))
+
+
+def way_tiles(df, dl, de):
+    if de or (df and dl):
+        return 1 if dl else 2
+    return 24 if df else 6
+
+
+PEERS = sorted(
+    ((df, de) for df in range(N_FIB) for de in range(N_EMG) if (df, de) != (0, 0)),
+    key=lambda peer: -hops(peer[0], 0, peer[1]),
+)
+AROUND = sorted(
+    [(0, 2, 0)] + [(df, dl, de) for df in (-1, 0, 1) for dl in (-1, 1) for de in (-1, 0, 1)],
+    key=lambda peer: -hops(*peer),
+)
 
 
 def cable_tables():
@@ -103,7 +128,7 @@
     s_in, s_work, s_new, lhs_ref, keep_ref, gain_b, wts_b, cur_ref, v1_ref, hot_ref, sel_ref,
     cell_send, cell_recv, row_send, row_recv, end_send, end_recv,
     own_ref, x_ref, r_ref, d_ref, t_ref, zr_ref, zd_ref, zt_ref, hz_ref,
-    y_send, z_send, wide_recv, z_recv,
+    y_send, z_send, e_send, wide_recv, z_recv, count_ref,
     in_sem, out_sem, small_sem, a2a_send, a2a_recv, len_send, len_recv, halo_ssem, halo_rsem,
 ):
     fib, shard, emg = lax.axis_index("fib"), lax.axis_index("len"), lax.axis_index("emg")
@@ -122,9 +147,10 @@
         copy.start()
     barrier = pltpu.get_barrier_semaphore()
 
-    def peer(step):
-        other = lax.rem(me + step, GROUPS)
-        return {"fib": other // N_EMG, "len": shard, "emg": lax.rem(other, N_EMG)}, other
+    def exists(df, dl, de):
+        steps = ((fib + df, N_FIB), (shard + dl, N_LEN), (emg + de, N_EMG))
+        inside = [(place >= 0) & (place < size) for place, size in steps]
+        return inside[0] & inside[1] & inside[2]
 
     def towards(df, dl, de):
         return {
@@ -133,25 +159,10 @@
             "emg": lax.rem(emg + N_EMG + de, N_EMG),
         }
 
-    def greet(step, _):
-        device, _other = peer(step)
-        pl.semaphore_signal(barrier, inc=1, device_id=device, device_id_type=MESH)
-        return 0
-
-    lax.fori_loop(1, GROUPS, greet, 0, unroll=UNROLL)
-    for step in range(1, N_LEN):
-        other = lax.rem(shard + step, N_LEN)
-        pl.semaphore_signal(
-            barrier, inc=1, device_id={"fib": fib, "len": other, "emg": emg}, device_id_type=MESH
-        )
-
-    for df in (-1, 0, 1):
-        for de in (-1, 0, 1):
-            for dl in (-1, 1):
-                if (df, de) != (0, 0):
-                    pl.semaphore_signal(
-                        barrier, inc=1, device_id=towards(df, dl, de), device_id_type=MESH
-                    )
+    for df, de in PEERS:
+        pl.semaphore_signal(barrier, inc=1, device_id=towards(df, 0, de), device_id_type=MESH)
+    for df, dl, de in AROUND:
+        pl.semaphore_signal(barrier, inc=1, device_id=towards(df, dl, de), device_id_type=MESH)
 
     s_in[:, pl.ds(STATES, ROWS - STATES), :] = jnp.zeros((NODES, ROWS - STATES, FIB), F32)
     quarter = NODES // 4
@@ -227,7 +238,7 @@
     )
     fire = dot(stim_row.astype(BF16), unit_hot.astype(BF16))
 
-    pl.semaphore_wait(barrier, GROUPS - 1 + N_LEN - 1 + 16)
+    pl.semaphore_wait(barrier, len(PEERS) + len(AROUND))
     node_id = shard * NODES + iota((NODES, FIB), 0)
     total_nodes = NODES * N_LEN
     band = (node_id >= total_nodes // 2 - band_half) & (node_id < total_nodes // 2 + band_half)
@@ -289,15 +300,13 @@
         return total.reshape(GROUPS, SLOT_ROWS, FIB)
 
     def exchange(source, target, slot_index):
-        def send(step, _):
-            device, other = peer(step)
+        for df, de in PEERS:
+            device = towards(df, 0, de)
+            other = device["fib"] * N_EMG + device["emg"]
             pltpu.make_async_remote_copy(
                 source.at[other], target.at[me], a2a_send.at[slot_index], a2a_recv.at[slot_index],
                 device_id=device, device_id_type=MESH,
             ).start()
-            return 0
-
-        lax.fori_loop(1, GROUPS, send, 0, unroll=UNROLL)
         target[me] = source[me]
 
     def exchange_wait(target, slot_index):
@@ -327,9 +336,12 @@
     def inside(condition):
         return jnp.where(condition, 1.0, 0.0).astype(F32)
 
-    fib_up, fib_down = inside(fib < N_FIB - 1), inside(fib > 0)
-    len_up, len_down = inside(shard < N_LEN - 1), inside(shard > 0)
-    emg_up, emg_down = inside(emg < N_EMG - 1), inside(emg > 0)
+    has_fib_up, has_fib_down = fib < N_FIB - 1, fib > 0
+    has_len_up, has_len_down = shard < N_LEN - 1, shard > 0
+    has_emg_up, has_emg_down = emg < N_EMG - 1, emg > 0
+    fib_up, fib_down = inside(has_fib_up), inside(has_fib_down)
+    len_up, len_down = inside(has_len_up), inside(has_len_down)
+    emg_up, emg_down = inside(has_emg_up), inside(has_emg_down)
     margin = jnp.where(sub < 4, fib_up, fib_down)
     zmask = jnp.where(zsub < 4, emg_up, emg_down)
     zmask = zmask * jnp.where(zlane < 256, 1.0, jnp.where(zlane < 320, len_up, len_down))
@@ -341,84 +353,110 @@
             turned = flat[tile * BZ : (tile + 1) * BZ, :].T
             z_send[kind, 0, tile] = turned[:4]
             z_send[kind, 1, tile] = turned[BZ - 4 :]
+        for f in range(2):
+            for x in range(2):
+                for k in range(2):
+                    rows = own[x * (BINS - 2) + k, f * (BY - 2) : f * (BY - 2) + 2, :]
+                    e_send[kind, f, x, 2 * k : 2 * k + 2, :] = rows
         for y in range(3):
             y_send[kind, 0, y * BINS : (y + 1) * BINS, :] = flat[pl.ds(y, BINS, stride=BY), :]
             y_send[kind, 1, y * BINS : (y + 1) * BINS, :] = flat[pl.ds(BY - 3 + y, BINS, stride=BY), :]
 
-        def post(source, target, sem, device):
-            pltpu.make_async_remote_copy(
-                source, target, halo_ssem.at[kind, sem], halo_rsem.at[kind, sem],
-                device_id=device, device_id_type=MESH,
-            ).start()
-
-        wide, tiles = wide_recv.at[kind], z_recv.at[kind]
-        for half, de in ((0, -1), (1, 1)):
-            base = 12 * half
-            for f, df in enumerate((-1, 1)):
-                for x, dl in enumerate((-1, 1)):
-                    post(
-                        z_send.at[kind, half, pl.ds(x, 1)],
-                        tiles.at[pl.ds(base + 8 + 2 * f + x, 1)], 1, towards(df, dl, de),
-                    )
-            for f, df in enumerate((-1, 1)):
-                post(
-                    z_send.at[kind, half], tiles.at[pl.ds(base + 4 + 2 * f, 2)], 1, towards(df, 0, de)
-                )
-            for x, dl in enumerate((-1, 1)):
-                post(
-                    z_send.at[kind, half, pl.ds(x, 1)], tiles.at[pl.ds(base + 2 + x, 1)], 1,
-                    towards(0, dl, de),
-                )
-            post(z_send.at[kind, half], tiles.at[pl.ds(base, 2)], 1, towards(0, 0, de))
-        for f, df in enumerate((-1, 1)):
-            for x, dl in enumerate((-1, 1)):
-                post(
-                    flat.at[pl.ds(x * (BINS - 2) * BY, 2 * BY)],
-                    wide.at[pl.ds(240 + 32 * f + 16 * x, 16)], 0, towards(df, dl, 0),
-                )
-        post(y_send.at[kind, 0], wide.at[pl.ds(96, 96)], 0, towards(-1, 0, 0))
-        post(y_send.at[kind, 1], wide.at[pl.ds(0, 96)], 0, towards(1, 0, 0))
-        post(flat.at[pl.ds(0, 24)], wide.at[pl.ds(216, 24)], 0, towards(0, -1, 0))
-        post(flat.at[pl.ds((BINS - 3) * BY, 24)], wide.at[pl.ds(192, 24)], 0, towards(0, 1, 0))
+        for way in WAYS:
+            source = margin_source(kind, flat, way)
+            target = margin_target(kind, tuple(-step for step in way))
+            copy = pltpu.make_async_remote_copy(
+                source, target, halo_ssem.at[kind], halo_rsem.at[kind],
+                device_id=towards(*way), device_id_type=MESH,
+            )
+            pl.when(exists(*way))(copy.start)
+
+    def margin_source(kind, flat, way):
+        df, dl, de = way
+        if de:
+            half = z_send.at[kind, max(de, 0)]
+            return half.at[pl.ds(max(dl, 0), 1)] if dl else half
+        if df and dl:
+            return e_send.at[kind, max(df, 0), pl.ds(max(dl, 0), 1)]
+        if df:
+            return y_send.at[kind, max(df, 0)]
+        return flat.at[pl.ds(0 if dl < 0 else (BINS - 3) * BY, 24)]
+
+    def margin_target(kind, way):
+        df, dl, de = way
+        f, x = int(df < 0), int(dl < 0)
+        if de:
+            base = 12 * int(de < 0)
+            if df and dl:
+                return z_recv.at[kind, pl.ds(base + 8 + 2 * f + x, 1)]
+            if dl:
+                return z_recv.at[kind, pl.ds(base + 2 + x, 1)]
+            return z_recv.at[kind, pl.ds(base + (4 + 2 * f if df else 0), 2)]
+        if df and dl:
+            return z_recv.at[kind, pl.ds(24 + 2 * f + x, 1)]
+        if df:
+            return wide_recv.at[kind, pl.ds(0 if df < 0 else 96, 96)]
+        return wide_recv.at[kind, pl.ds(192 if dl < 0 else 216, 24)]
+
+    at_edge = [
+        (place == 0) | (place == size - 1)
+        for place, size in ((fib, N_FIB), (shard, N_LEN), (emg, N_EMG))
+    ]
+
+    def margins_wait(kind, sem):
+        for edges in itertools.product((False, True), repeat=3):
+            ways = [
+                way for way in WAYS
+                if not any(edge and step < 0 for edge, step in zip(edges, way))
+            ]
+            tiles = sum(way_tiles(*way) for way in ways)
+            here = [at == edge for at, edge in zip(at_edge, edges)]
+            whole = count_ref.at[pl.ds(0, tiles)]
+            copy = pltpu.make_async_copy(whole, whole, sem.at[kind])
+            pl.when(here[0] & here[1] & here[2])(copy.wait)
 
     def assemble(kind, own, field, zfield, add):
+        def only(condition, values):
+            return jnp.where(condition, values, 0.0)
+
         def plus(values):
             return values + add if add else values
 
         wide, tiles = wide_recv.at[kind], z_recv.at[kind]
-        pltpu.make_async_copy(wide, wide, halo_rsem.at[kind, 0]).wait()
-        pltpu.make_async_copy(tiles, tiles, halo_rsem.at[kind, 1]).wait()
+        margins_wait(kind, halo_rsem)
         field[0, pl.ds(0, BINS)] = plus(own[...])
         for k in range(3):
-            field[0, BINS + k] = plus(wide[216 + 8 * k : 224 + 8 * k, :] * len_up)
-            field[0, WRAP - 3 + k] = plus(wide[192 + 8 * k : 200 + 8 * k, :] * len_down)
+            field[0, BINS + k] = plus(only(has_len_up, wide[216 + 8 * k : 224 + 8 * k, :]))
+            field[0, WRAP - 3 + k] = plus(only(has_len_down, wide[192 + 8 * k : 200 + 8 * k, :]))
         beside = field.at[1].reshape(WRAP * BY, BZ)
         for y in range(3):
-            beside[pl.ds(y, BINS, stride=BY), :] = plus(wide[96 + 32 * y : 128 + 32 * y, :] * fib_up)
-            beside[pl.ds(BY - 3 + y, BINS, stride=BY), :] = plus(wide[32 * y : 32 * y + 32, :] * fib_down)
-        for k in range(2):
-            for x, (place, weight) in enumerate(((BINS, len_up), (WRAP - 2, len_down))):
-                start = 240 + 16 * x + 8 * k
-                up, down = wide[start : start + 8, :], wide[start + 32 : start + 40, :]
-                edge = jnp.where(sub < 4, up * fib_up, down * fib_down)
-                field[1, place + k] = plus(edge * weight)
+            beside[pl.ds(y, BINS, stride=BY), :] = plus(only(has_fib_up, wide[96 + 32 * y : 128 + 32 * y, :]))
+            beside[pl.ds(BY - 3 + y, BINS, stride=BY), :] = plus(only(has_fib_down, wide[32 * y : 32 * y + 32, :]))
+        for f, along in enumerate((has_fib_up, has_fib_down)):
+            for x, (place, weight) in enumerate(((BINS, has_len_up), (WRAP - 2, has_len_down))):
+                for k in range(2):
+                    rows = tiles[24 + 2 * f + x, 2 * k : 2 * k + 2, :]
+                    field[1, place + k, f * (BY - 2) : f * (BY - 2) + 2, :] = plus(
+                        only(along & weight, rows)
+                    )
         low = iota((4, BZ), 1) < BZ // 2
         near = lax.rem(iota((4, BZ), 1), BY) < 4
-        for half, weight in ((0, emg_up), (1, emg_down)):
+        for half, weight in ((0, has_emg_up), (1, has_emg_down)):
             base = 12 * half
             rows = slice(4 * half, 4 * half + 4)
             for tile in range(2):
                 lanes = slice(tile * BZ, (tile + 1) * BZ)
-                zfield[0, rows, lanes] = plus(tiles[base + tile] * weight)
-                up, down = tiles[base + 4 + tile] * fib_up, tiles[base + 6 + tile] * fib_down
-                zfield[1, rows, lanes] = plus(jnp.where(near, up, down) * weight)
+                zfield[0, rows, lanes] = plus(only(weight, tiles[base + tile]))
+                up = only(has_fib_up, tiles[base + 4 + tile])
+                down = only(has_fib_down, tiles[base + 6 + tile])
+                zfield[1, rows, lanes] = plus(only(weight, jnp.where(near, up, down)))
             lanes = slice(2 * BZ, 3 * BZ)
-            both = jnp.where(low, tiles[base + 2] * len_up, tiles[base + 3] * len_down)
-            zfield[0, rows, lanes] = plus(both * weight)
-            up = jnp.where(low, tiles[base + 8] * len_up, tiles[base + 9] * len_down)
-            down = jnp.where(low, tiles[base + 10] * len_up, tiles[base + 11] * len_down)
-            both = jnp.where(near, up * fib_up, down * fib_down)
-            zfield[1, rows, lanes] = plus(both * weight)
+            both = jnp.where(low, only(has_len_up, tiles[base + 2]), only(has_len_down, tiles[base + 3]))
+            zfield[0, rows, lanes] = plus(only(weight, both))
+            up = jnp.where(low, only(has_len_up, tiles[base + 8]), only(has_len_down, tiles[base + 9]))
+            down = jnp.where(low, only(has_len_up, tiles[base + 10]), only(has_len_down, tiles[base + 11]))
+            both = jnp.where(near, only(has_fib_up, up), only(has_fib_down, down))
+            zfield[1, rows, lanes] = plus(only(weight, both))
 
     def scatter(step):
         exchange_wait(row_recv.at[step], 1 + step)
@@ -444,7 +482,7 @@
         zfield = zr_ref.at[step] if first else zd_ref.at[step]
         blank = jnp.zeros((BZ - 16, BZ), F32)
         for tile in range(1 if last else 2):
-            for block in range(2 if last else 3):
+            for block in range(2 if last or (turn and tile) else 3):
                 z = zfield[tile, :, block * BZ : (block + 1) * BZ]
                 first_lane = jnp.where(sub == 0, pltpu.roll(z, 1, 0), 0.0)
                 last_lane = jnp.where(sub == 7, pltpu.roll(z, 7, 0), 0.0)
@@ -460,37 +498,41 @@
 
         if not last:
             zs = [zfield[0], zfield[1]]
-            edges = []
-            for t in range(2):
-                parts = []
-                for block in range(3):
-                    turned = field[t, pl.ds(16 * block, 16)].reshape(BZ, BZ).T
-                    ends = jnp.where(
-                        sub == 0, pltpu.roll(turned[BZ - 8 :], 1, 0), pltpu.roll(turned[:8], 7, 0)
-                    )
-                    parts.append(ends)
-                edges.append(jnp.concatenate(parts, axis=1))
             up = [pltpu.roll(z, 1, 1) for z in zs]
             down = [pltpu.roll(z, WRAP * BY - 1, 1) for z in zs]
             up_far = [pltpu.roll(z, WRAP * BY - BY + 1, 1) for z in zs]
             down_far = [pltpu.roll(z, BY - 1, 1) for z in zs]
-            for t in range(2):
+            for t in range(1 if turn else 2):
+                blocks = 2 if turn or t else 3
+                width = blocks * BZ
+                ends = []
+                for block in range(blocks):
+                    turned = field[t, pl.ds(16 * block, 16)].reshape(BZ, BZ).T
+                    ends.append(
+                        jnp.where(
+                            sub == 0, pltpu.roll(turned[BZ - 8 :], 1, 0), pltpu.roll(turned[:8], 7, 0)
+                        )
+                    )
+                edges = jnp.concatenate(ends, axis=1)
                 beside = pltpu.roll(zs[t], BY, 1) + pltpu.roll(zs[t], WRAP * BY - BY, 1)
                 beside = beside + jnp.where(zrow == 0, up_far[1 - t], up[t])
                 beside = beside + jnp.where(zrow == BY - 1, down_far[1 - t], down[t])
-                beside = beside + jnp.where(zsub == 0, edges[t], pltpu.roll(zs[t], 1, 0))
-                beside = beside + jnp.where(zsub == 7, edges[t], pltpu.roll(zs[t], 7, 0))
+                row, beside = zsub[:, :width], beside[:, :width]
+                z = zs[t][:, :width]
+                beside = beside + jnp.where(row == 0, edges, pltpu.roll(z, 1, 0))
+                beside = beside + jnp.where(row == 7, edges, pltpu.roll(z, 7, 0))
                 rest, after = advance(
-                    zs[t], beside, zt_ref[t], None if first else zr_ref[step, t], gain * zmasks[t]
+                    z, beside, zt_ref[t, :, :width], None if first else zr_ref[step, t, :, :width],
+                    gain * zmasks[t][:, :width],
                 )
-                zr_ref[step, t] = rest
-                zd_ref[step, t] = after
-
-        def slab(place, following, previous, push, own):
+                zr_ref[step, t, :, :width] = rest
+                zd_ref[step, t, :, :width] = after
+
+        def slab(place, following, previous, push, own, tiles=2):
             here = (field[0, place], field[1, place])
             up = [pltpu.roll(h, 1, 0) for h in here]
             down = [pltpu.roll(h, BY - 1, 0) for h in here]
-            for t in range(1 if last else 2):
+            for t in range(1 if last else tiles):
                 beside = previous[t] + field[t, following] + hz_ref[t, place]
                 beside = beside + jnp.where(sub == 0, up[1 - t], up[t])
                 beside = beside + jnp.where(sub == BY - 1, down[1 - t], down[t])
@@ -517,12 +559,14 @@
         previous = (field[0, start], field[1, start])
         for k in range(reach):
             place = start + 1 + k
-            previous = slab(place, (place + 1) % WRAP, previous, gain * len_down, False)
+            tiles = 2 if k else 1
+            previous = slab(place, (place + 1) % WRAP, previous, gain * len_down, False, tiles)
         previous = lax.fori_loop(
             0, BINS, lambda x, before: slab(x, x + 1, before, gain, True), previous, unroll=32
         )
         for k in range(reach):
-            previous = slab(BINS + k, BINS + k + 1, previous, gain * len_up, False)
+            tiles = 2 if k + 1 < reach else 1
+            previous = slab(BINS + k, BINS + k + 1, previous, gain * len_up, False, tiles)
 
     spread_out(STEPS, tissue_ref)
     r_ref[...] = jnp.zeros_like(r_ref)
@@ -561,23 +605,25 @@
 
     lax.fori_loop(0, NODES, put, 0, unroll=16)
     assemble(STEPS, tissue_ref, t_ref, zt_ref, 6.0)
+    exchange_sent(cell_send, 0)
+    margins_wait(STEPS, halo_ssem)
     volt_out[...] = cable_end(1, local)
     scatter(1)
     spread_out(1, own_ref.at[1])
+    def sent(step):
+        exchange_sent(row_send.at[step], 1 + step)
+        whole = end_recv.at[step, pl.ds(0, N_LEN - 1)]
+        pltpu.make_async_copy(whole, whole, len_send.at[step]).wait()
+        margins_wait(step, halo_ssem)
+
     for step in range(STEPS):
+        if step:
+            pltpu.make_async_copy(states_out, states_out, out_sem.at[0]).wait()
+            sent(0)
+            sent(1)
         assemble(step, own_ref.at[step], r_ref.at[step], zr_ref.at[step], 0.0)
         for turn in range(SWEEPS - 1):
             sweep(step, turn)
-
-    pltpu.make_async_copy(states_out, states_out, out_sem.at[0]).wait()
-    exchange_sent(cell_send, 0)
-    for step in range(STEPS):
-        exchange_sent(row_send.at[step], 1 + step)
-        whole = end_recv.at[step, pl.ds(0, N_LEN - 1)]
-        pltpu.make_async_copy(whole, whole, len_send.at[step]).wait()
-    for kind in range(STEPS + 1):
-        for number, sent in enumerate((wide_recv.at[kind], z_recv.at[kind])):
-            pltpu.make_async_copy(sent, sent, halo_ssem.at[kind, number]).wait()
 
 
 def write_out(states, voltage, potential, states_out, voltage_out, potential_out, sem):
@@ -655,8 +701,10 @@
             pltpu.VMEM((2, WRAP, BY, BZ), F32),
             pltpu.VMEM((STEPS + 1, 2, 3 * BINS, BZ), F32),
             pltpu.VMEM((STEPS + 1, 2, 2, 4, BZ), F32),
+            pltpu.VMEM((STEPS + 1, 2, 2, 4, BZ), F32),
             pltpu.VMEM((STEPS + 1, WIDE_ROWS, BZ), F32),
-            pltpu.VMEM((STEPS + 1, Z_TILES, 4, BZ), F32),
+            pltpu.VMEM((STEPS + 1, TILES, 4, BZ), F32),
+            pltpu.VMEM((WIDE_ROWS // 4 + TILES, 4, BZ), F32),
             pltpu.SemaphoreType.DMA((4,)),
             pltpu.SemaphoreType.DMA((1,)),
             pltpu.SemaphoreType.DMA((12,)),
@@ -664,8 +712,8 @@
             pltpu.SemaphoreType.DMA((3,)),
             pltpu.SemaphoreType.DMA((STEPS,)),
             pltpu.SemaphoreType.DMA((STEPS,)),
-            pltpu.SemaphoreType.DMA((STEPS + 1, 2)),
-            pltpu.SemaphoreType.DMA((STEPS + 1, 2)),
+            pltpu.SemaphoreType.DMA((STEPS + 1,)),
+            pltpu.SemaphoreType.DMA((STEPS + 1,)),
         ],
         compiler_params=pltpu.CompilerParams(collective_id=0, has_side_effects=True, vmem_limit_bytes=VMEM_LIMIT),
     )(*(pltpu.with_memory_space_constraint(array, pltpu.HBM) for array in (

time: 27.3 us -> 25.2 us (0.923)
  Pallas kernels: 26.5 us -> 24.3 us
    pallas_call x1, Pallas kernels: 25 us -> 23 us  [on_device(): pl.pallas_call(kernel, out_shape=(jax.ShapeDtypeStruct(states.shape, F32)...]
where the time goes in v5:
time: 25.2 us; the launch traced here: 25 us
  Pallas kernels  24.3 us (96%)
  between operations  0.64 us (3%)
    pallas_call x1, Pallas kernels, on_device(): pl.pallas_call(kernel, out_shape=(jax.ShapeDtypeStruct(states.shape, F32)...  23 us
    pallas_call x1, Pallas kernels, on_device(): pl.pallas_call(write_out, out_shape=tuple((jax.ShapeDtypeStruct(array.sha...  1.37 us

profile of v5, /device:TPU:1, one launch (start us, length us, event | category | flops | bytes accessed | tf_op | source)
XLA Modules:
  0.0 25.0 jit_solution(2646251691382270475)
XLA Ops:
  0.6 23.0 %shard_map.148 = (f32[57,64,128]{2,1,0:T(8,128)S(1)}, f32[64,128]{1,0:T(8,128)S(1)}, f32[2,32,8,128]{3,2,1,0:T(8,128)S(1)}) custom-call(f32[57,64,128]{2,1,0:T(8,128)} %states_hbm.1, f32[64,128]{1,0:T(8,128)} %volt_hbm.1, f32[57,57]{1,0:T(8,128)} %coup_hbm.1, f32[1,57]{1,0:T(1,128)} %bitcast.7, f32[1,57]{1,0:T(1,128)} %bitcast.8, f32[1,57]{1,0:T(1,128)} %bitcast.9, ...), custom_call_target="tpu_custom_call" | custom-call | tf_op jit(solution)/shard_map/pallas_call | solution.py:654
  23.6 1.4 %shard_map.149 = (f32[57,64,128]{2,1,0:T(8,128)}, f32[64,128]{1,0:T(8,128)}, f32[2,32,8,128]{3,2,1,0:T(8,128)}) custom-call(f32[57,64,128]{2,1,0:T(8,128)S(1)} %get-tuple-element.6.states, f32[64,128]{1,0:T(8,128)S(1)} %get-tuple-element.7.voltage, f32[2,32,8,128]{3,2,1,0:T(8,128)S(1)} %get-tuple-element.8.potential), custom_call_target="tpu_custom_call" | custom-call | tf_op jit(solution)/shard_map/pallas_call | solution.py:724

commit v6 on v5

--- a/solution.py
+++ b/solution.py
@@ -61,8 +61,10 @@
     ((df, de) for df in range(N_FIB) for de in range(N_EMG) if (df, de) != (0, 0)),
     key=lambda peer: -hops(peer[0], 0, peer[1]),
 )
-AROUND = sorted(
-    [(0, 2, 0)] + [(df, dl, de) for df in (-1, 0, 1) for dl in (-1, 1) for de in (-1, 0, 1)],
+AXIS_PEERS = sorted(
+    [(step, 0, 0) for step in range(1, N_FIB)]
+    + [(0, step, 0) for step in range(1, N_LEN)]
+    + [(0, 0, step) for step in range(1, N_EMG)],
     key=lambda peer: -hops(*peer),
 )
 
@@ -74,20 +76,14 @@
     u = np.array([math.cosh((i + 0.5) * theta) for i in range(total)])
     v = np.array([math.cosh((total - 0.5 - i) * theta) / scale for i in range(total)])
     index = np.arange(NODES)
-    local = np.zeros((N_LEN, NODES + 8, NODES))
-    far = np.zeros((N_LEN, NODES, 8 * N_LEN))
+    local = np.zeros((N_LEN, NODES, NODES))
+    ends = np.zeros((N_LEN, 2, NODES, FIB))
     for shard in range(N_LEN):
         us, vs = u[shard * NODES :][:NODES], v[shard * NODES :][:NODES]
         low = index[:, None] <= index[None, :]
-        local[shard, :NODES] = np.where(low, us[:, None] * vs[None, :], vs[:, None] * us[None, :])
-        local[shard, NODES] = us
-        local[shard, NODES + 1] = vs
-        for other in range(N_LEN):
-            if other < shard:
-                far[shard, :, 8 * other] = vs
-            if other > shard:
-                far[shard, :, 8 * other + 1] = us
-    return jnp.asarray(local, F32), jnp.asarray(far, F32)
+        local[shard] = np.where(low, us[:, None] * vs[None, :], vs[:, None] * us[None, :])
+        ends[shard] = np.stack([us, vs])[:, :, None]
+    return jnp.asarray(local, F32), jnp.asarray(ends, F32)
 
 
 def iota(shape, axis):
@@ -126,10 +122,10 @@
     volt_ref, coup_ref, decay_ref, gain_ref, wts_ref, home_ref, cell_ref, mu_ref,
     stim_ref, tissue_ref, local_ref, far_ref,
     s_in, s_work, s_new, lhs_ref, keep_ref, gain_b, wts_b, cur_ref, v1_ref, hot_ref, sel_ref,
-    cell_send, cell_recv, row_send, row_recv, end_send, end_recv,
+    cell_send, cell_recv, row_send, row_recv, ends_out, ends_in,
     own_ref, x_ref, r_ref, d_ref, t_ref, zr_ref, zd_ref, zt_ref, hz_ref,
     y_send, z_send, e_send, wide_recv, z_recv, count_ref,
-    in_sem, out_sem, small_sem, a2a_send, a2a_recv, len_send, len_recv, halo_ssem, halo_rsem,
+    in_sem, out_sem, small_sem, a2a_send, a2a_recv, len_send, len_recv, halo_ssem, halo_rsem, entered,
 ):
     fib, shard, emg = lax.axis_index("fib"), lax.axis_index("len"), lax.axis_index("emg")
     me = fib * N_EMG + emg
@@ -139,7 +135,7 @@
         for number, (source, target) in enumerate((
             (coup_hbm, coup_ref), (decay_hbm, decay_ref), (gain_hbm, gain_ref), (wts_hbm, wts_ref),
             (home_hbm, home_ref), (cell_hbm, cell_ref), (mu_hbm, mu_ref), (stim_hbm, stim_ref),
-            (volt_hbm, volt_ref), (local_hbm, local_ref), (far_hbm, far_ref),
+            (volt_hbm, volt_ref), (local_hbm.at[shard], local_ref), (far_hbm.at[shard], far_ref),
             (tissue_hbm, tissue_ref),
         ))
     ]
@@ -159,10 +155,8 @@
             "emg": lax.rem(emg + N_EMG + de, N_EMG),
         }
 
-    for df, de in PEERS:
-        pl.semaphore_signal(barrier, inc=1, device_id=towards(df, 0, de), device_id_type=MESH)
-    for df, dl, de in AROUND:
-        pl.semaphore_signal(barrier, inc=1, device_id=towards(df, dl, de), device_id_type=MESH)
+    for way in AXIS_PEERS:
+        pl.semaphore_signal(barrier, inc=1, device_id=towards(*way), device_id_type=MESH)
 
     s_in[:, pl.ds(STATES, ROWS - STATES), :] = jnp.zeros((NODES, ROWS - STATES, FIB), F32)
     quarter = NODES // 4
@@ -238,7 +232,7 @@
     )
     fire = dot(stim_row.astype(BF16), unit_hot.astype(BF16))
 
-    pl.semaphore_wait(barrier, len(PEERS) + len(AROUND))
+    pl.semaphore_wait(barrier, len(AXIS_PEERS))
     node_id = shard * NODES + iota((NODES, FIB), 0)
     total_nodes = NODES * N_LEN
     band = (node_id >= total_nodes // 2 - band_half) & (node_id < total_nodes // 2 + band_half)
@@ -247,22 +241,24 @@
         active = (fire == float(step)).astype(F32)
         pulse = jnp.where(band, amplitude * active, 0.0)
         right = volts + time_step * (pulse - cur_ref[...])
-        both = dot_high(local_ref[shard], right)
-        end_send[step] = both[NODES:]
+        ends_out[step, 0:1, :] = jnp.sum(far_ref[0] * right, axis=0, keepdims=True)
+        ends_out[step, 1:2, :] = jnp.sum(far_ref[1] * right, axis=0, keepdims=True)
         for other_step in range(1, N_LEN):
             other = lax.rem(shard + other_step, N_LEN)
             pltpu.make_async_remote_copy(
-                end_send.at[step], end_recv.at[step, shard], len_send.at[step], len_recv.at[step],
+                ends_out.at[step], ends_in.at[step, shard], len_send.at[step], len_recv.at[step],
                 device_id={"fib": fib, "len": other, "emg": emg}, device_id_type=MESH,
             ).start()
-        end_recv[step, shard] = jnp.zeros((8, FIB), F32)
-        return both[:NODES]
+        return dot_high(local_ref[...], right)
 
     def cable_end(step, local):
-        whole = end_recv.at[step, pl.ds(0, N_LEN - 1)]
+        whole = ends_in.at[step, pl.ds(0, N_LEN - 1)]
         pltpu.make_async_copy(whole, whole, len_recv.at[step]).wait()
-        far = end_recv[step].reshape(8 * N_LEN, FIB)
-        return local + dot_high(far_ref[shard], far)
+        below = above = jnp.zeros((1, FIB), F32)
+        for other in range(N_LEN):
+            below = below + jnp.where(other < shard, ends_in[step, other, 0:1, :], 0.0)
+            above = above + jnp.where(other > shard, ends_in[step, other, 1:2, :], 0.0)
+        return local + far_ref[1] * below + far_ref[0] * above
 
     def binned():
         first = cur_ref[pl.ds(0, BINS, stride=2), :]
@@ -270,6 +266,8 @@
         return first + second
 
     local = cable_begin(0, volt_ref[...])
+    for df in range(1, N_FIB):
+        pl.semaphore_signal(entered, inc=1, device_id=towards(df, 0, 0), device_id_type=MESH)
     home = home_ref[...]
     member = (iota((GROUPS, FIB), 0) == home).astype(F32)
     before = (iota((FIB, FIB), 0) < iota((FIB, FIB), 1)).astype(BF16)
@@ -320,9 +318,7 @@
     cell_row = jnp.broadcast_to(cell_ref[...].astype(F32), (BINS, FIB))
     cell_send[...] = pack(cell_row)
 
-    exchange(cell_send, cell_recv, 0)
     row_send[0] = pack(binned())
-    exchange(row_send.at[0], row_recv.at[0], 1)
 
     middle = 0.5 * (high_bound + low_bound)
     spread_width = 0.5 * (high_bound - low_bound)
@@ -568,11 +564,13 @@
             tiles = 2 if k + 1 < reach else 1
             previous = slab(BINS + k, BINS + k + 1, previous, gain * len_up, False, tiles)
 
-    spread_out(STEPS, tissue_ref)
     r_ref[...] = jnp.zeros_like(r_ref)
     d_ref[...] = jnp.zeros_like(d_ref)
     t_ref[...] = jnp.zeros_like(t_ref)
     lax.fori_loop(0, NODES // 2, next_pair, 0, unroll=8)
+    pl.semaphore_wait(entered, N_FIB - 1)
+    exchange(cell_send, cell_recv, 0)
+    exchange(row_send.at[0], row_recv.at[0], 1)
     v1_ref[...] = cable_end(0, local)
 
     def second(node, _):
@@ -586,6 +584,14 @@
     row_send[1] = pack(binned())
     exchange(row_send.at[1], row_recv.at[1], 2)
     local = cable_begin(1, v1_ref[...])
+
+    def put(node, _):
+        pltpu.make_async_copy(
+            s_in.at[node, pl.ds(0, STATES), :], states_out.at[:, node, :], out_sem.at[0]
+        ).start()
+        return 0
+
+    lax.fori_loop(0, NODES, put, 0, unroll=16)
 
     exchange_wait(cell_recv, 0)
     cells = cell_recv[...].reshape(packed, FIB)
@@ -597,27 +603,22 @@
 
     scatter(0)
     spread_out(0, own_ref.at[0])
-    def put(node, _):
-        pltpu.make_async_copy(
-            s_in.at[node, pl.ds(0, STATES), :], states_out.at[:, node, :], out_sem.at[0]
-        ).start()
-        return 0
-
-    lax.fori_loop(0, NODES, put, 0, unroll=16)
-    assemble(STEPS, tissue_ref, t_ref, zt_ref, 6.0)
+    spread_out(STEPS, tissue_ref)
     exchange_sent(cell_send, 0)
-    margins_wait(STEPS, halo_ssem)
     volt_out[...] = cable_end(1, local)
     scatter(1)
     spread_out(1, own_ref.at[1])
     def sent(step):
         exchange_sent(row_send.at[step], 1 + step)
-        whole = end_recv.at[step, pl.ds(0, N_LEN - 1)]
+        whole = ends_in.at[step, pl.ds(0, N_LEN - 1)]
         pltpu.make_async_copy(whole, whole, len_send.at[step]).wait()
         margins_wait(step, halo_ssem)
 
     for step in range(STEPS):
-        if step:
+        if step == 0:
+            assemble(STEPS, tissue_ref, t_ref, zt_ref, 6.0)
+            margins_wait(STEPS, halo_ssem)
+        else:
             pltpu.make_async_copy(states_out, states_out, out_sem.at[0]).wait()
             sent(0)
             sent(1)
@@ -671,8 +672,8 @@
             pltpu.VMEM((1, FIB), jnp.int32),
             pltpu.VMEM((1, stim_step.shape[0]), jnp.int32),
             pltpu.VMEM(tissue.shape, F32),
-            pltpu.VMEM(local.shape, F32),
-            pltpu.VMEM(far.shape, F32),
+            pltpu.VMEM(local.shape[1:], F32),
+            pltpu.VMEM(far.shape[1:], F32),
             pltpu.VMEM((NODES, ROWS, FIB), F32),
             pltpu.VMEM((NODES, ROWS, FIB), F32),
             pltpu.VMEM((NODES, ROWS, FIB), F32),
@@ -688,8 +689,8 @@
             pltpu.VMEM((GROUPS, SLOT_ROWS, FIB), F32),
             pltpu.VMEM((STEPS, GROUPS, SLOT_ROWS, FIB), F32),
             pltpu.VMEM((STEPS, GROUPS, SLOT_ROWS, FIB), F32),
-            pltpu.VMEM((STEPS, 8, FIB), F32),
-            pltpu.VMEM((STEPS, N_LEN, 8, FIB), F32),
+            pltpu.VMEM((STEPS, 2, FIB), F32),
+            pltpu.VMEM((STEPS, N_LEN, 2, FIB), F32),
             pltpu.VMEM((STEPS, BINS, BY, BZ), F32),
             pltpu.VMEM((STEPS, BINS, BY, BZ), F32),
             pltpu.VMEM((STEPS, 2, WRAP, BY, BZ), F32),
@@ -714,6 +715,7 @@
             pltpu.SemaphoreType.DMA((STEPS,)),
             pltpu.SemaphoreType.DMA((STEPS + 1,)),
             pltpu.SemaphoreType.DMA((STEPS + 1,)),
+            pltpu.SemaphoreType.REGULAR,
         ],
         compiler_params=pltpu.CompilerParams(collective_id=0, has_side_effects=True, vmem_limit_bytes=VMEM_LIMIT),
     )(*(pltpu.with_memory_space_constraint(array, pltpu.HBM) for array in (

time: 25.2 us -> 24.5 us (0.972)
  Pallas kernels: 24.3 us -> 23.8 us
    pallas_call x1, Pallas kernels: 23 us -> 22.4 us  [on_device(): pl.pallas_call(kernel, out_shape=(jax.ShapeDtypeStruct(states.shape, F32)...]
where the time goes in v6:
time: 24.5 us; the launch traced here: 24.4 us
  Pallas kernels  23.8 us (97%)
  between operations  0.64 us (3%)
    pallas_call x1, Pallas kernels, on_device(): pl.pallas_call(kernel, out_shape=(jax.ShapeDtypeStruct(states.shape, F32)...  22.4 us
    pallas_call x1, Pallas kernels, on_device(): pl.pallas_call(write_out, out_shape=tuple((jax.ShapeDtypeStruct(array.sha...  1.37 us

profile of v6, /device:TPU:1, one launch (start us, length us, event | category | flops | bytes accessed | tf_op | source)
XLA Modules:
  0.0 24.4 jit_solution(12919973424123205032)
XLA Ops:
  0.6 22.4 %shard_map.148 = (f32[57,64,128]{2,1,0:T(8,128)S(1)}, f32[64,128]{1,0:T(8,128)S(1)}, f32[2,32,8,128]{3,2,1,0:T(8,128)S(1)}) custom-call(f32[57,64,128]{2,1,0:T(8,128)} %states_hbm.1, f32[64,128]{1,0:T(8,128)} %volt_hbm.1, f32[57,57]{1,0:T(8,128)} %coup_hbm.1, f32[1,57]{1,0:T(1,128)} %bitcast.7, f32[1,57]{1,0:T(1,128)} %bitcast.8, f32[1,57]{1,0:T(1,128)} %bitcast.9, ...), custom_call_target="tpu_custom_call" | custom-call | tf_op jit(solution)/shard_map/pallas_call | solution.py:655
  23.0 1.4 %shard_map.149 = (f32[57,64,128]{2,1,0:T(8,128)}, f32[64,128]{1,0:T(8,128)}, f32[2,32,8,128]{3,2,1,0:T(8,128)}) custom-call(f32[57,64,128]{2,1,0:T(8,128)S(1)} %get-tuple-element.6.states, f32[64,128]{1,0:T(8,128)S(1)} %get-tuple-element.7.voltage, f32[2,32,8,128]{3,2,1,0:T(8,128)S(1)} %get-tuple-element.8.potential), custom_call_target="tpu_custom_call" | custom-call | tf_op jit(solution)/shard_map/pallas_call | solution.py:726

commit v7 on v6

--- a/solution.py
+++ b/solution.py
@@ -122,7 +122,7 @@
     volt_ref, coup_ref, decay_ref, gain_ref, wts_ref, home_ref, cell_ref, mu_ref,
     stim_ref, tissue_ref, local_ref, far_ref,
     s_in, s_work, s_new, lhs_ref, keep_ref, gain_b, wts_b, cur_ref, v1_ref, hot_ref, sel_ref,
-    cell_send, cell_recv, row_send, row_recv, ends_out, ends_in,
+    both_send, both_recv, row_send, row_recv, ends_out, ends_in,
     own_ref, x_ref, r_ref, d_ref, t_ref, zr_ref, zd_ref, zt_ref, hz_ref,
     y_send, z_send, e_send, wide_recv, z_recv, count_ref,
     in_sem, out_sem, small_sem, a2a_send, a2a_recv, len_send, len_recv, halo_ssem, halo_rsem, entered,
@@ -316,9 +316,9 @@
         pltpu.make_async_copy(whole, whole, a2a_send.at[slot_index]).wait()
 
     cell_row = jnp.broadcast_to(cell_ref[...].astype(F32), (BINS, FIB))
-    cell_send[...] = pack(cell_row)
-
-    row_send[0] = pack(binned())
+    both_send[:, SLOT_ROWS:, :] = pack(cell_row)
+
+    both_send[:, :SLOT_ROWS, :] = pack(binned())
 
     middle = 0.5 * (high_bound + low_bound)
     spread_width = 0.5 * (high_bound - low_bound)
@@ -455,8 +455,10 @@
             zfield[1, rows, lanes] = plus(only(weight, both))
 
     def scatter(step):
-        exchange_wait(row_recv.at[step], 1 + step)
-        rows = row_recv[step].reshape(packed, FIB)
+        if step:
+            exchange_wait(row_recv, 1)
+        rows = row_recv[...] if step else both_recv[:, :SLOT_ROWS, :]
+        rows = rows.reshape(packed, FIB)
         turned = rows.T
         wide = jnp.concatenate([turned[q * BINS : (q + 1) * BINS] for q in range(4)], axis=1)
         both = dot(jnp.concatenate(split(wide), axis=0), hot_ref[...])
@@ -569,8 +571,7 @@
     t_ref[...] = jnp.zeros_like(t_ref)
     lax.fori_loop(0, NODES // 2, next_pair, 0, unroll=8)
     pl.semaphore_wait(entered, N_FIB - 1)
-    exchange(cell_send, cell_recv, 0)
-    exchange(row_send.at[0], row_recv.at[0], 1)
+    exchange(both_send, both_recv, 0)
     v1_ref[...] = cable_end(0, local)
 
     def second(node, _):
@@ -581,8 +582,8 @@
         return 0
 
     lax.fori_loop(0, NODES, second, 0, unroll=8)
-    row_send[1] = pack(binned())
-    exchange(row_send.at[1], row_recv.at[1], 2)
+    row_send[...] = pack(binned())
+    exchange(row_send, row_recv, 1)
     local = cable_begin(1, v1_ref[...])
 
     def put(node, _):
@@ -593,8 +594,8 @@
 
     lax.fori_loop(0, NODES, put, 0, unroll=16)
 
-    exchange_wait(cell_recv, 0)
-    cells = cell_recv[...].reshape(packed, FIB)
+    exchange_wait(both_recv, 0)
+    cells = both_recv[:, SLOT_ROWS:, :].reshape(packed, FIB)
     for q in range(4):
         column_q = cells[:, q * BINS : q * BINS + 1].astype(jnp.int32)
         for y in range(BY):
@@ -604,12 +605,11 @@
     scatter(0)
     spread_out(0, own_ref.at[0])
     spread_out(STEPS, tissue_ref)
-    exchange_sent(cell_send, 0)
     volt_out[...] = cable_end(1, local)
     scatter(1)
     spread_out(1, own_ref.at[1])
     def sent(step):
-        exchange_sent(row_send.at[step], 1 + step)
+        exchange_sent(row_send if step else both_send, step)
         whole = ends_in.at[step, pl.ds(0, N_LEN - 1)]
         pltpu.make_async_copy(whole, whole, len_send.at[step]).wait()
         margins_wait(step, halo_ssem)
@@ -685,10 +685,10 @@
             pltpu.VMEM((NODES, FIB), F32),
             pltpu.VMEM((4 * GROUPS * SLOT_ROWS, BY * BZ), BF16),
             pltpu.VMEM((GROUPS * SLOT_ROWS, 4 * FIB), BF16),
+            pltpu.VMEM((GROUPS, 2 * SLOT_ROWS, FIB), F32),
+            pltpu.VMEM((GROUPS, 2 * SLOT_ROWS, FIB), F32),
             pltpu.VMEM((GROUPS, SLOT_ROWS, FIB), F32),
             pltpu.VMEM((GROUPS, SLOT_ROWS, FIB), F32),
-            pltpu.VMEM((STEPS, GROUPS, SLOT_ROWS, FIB), F32),
-            pltpu.VMEM((STEPS, GROUPS, SLOT_ROWS, FIB), F32),
             pltpu.VMEM((STEPS, 2, FIB), F32),
             pltpu.VMEM((STEPS, N_LEN, 2, FIB), F32),
             pltpu.VMEM((STEPS, BINS, BY, BZ), F32),
@@ -709,8 +709,8 @@
             pltpu.SemaphoreType.DMA((4,)),
             pltpu.SemaphoreType.DMA((1,)),
             pltpu.SemaphoreType.DMA((12,)),
-            pltpu.SemaphoreType.DMA((3,)),
-            pltpu.SemaphoreType.DMA((3,)),
+            pltpu.SemaphoreType.DMA((STEPS,)),
+            pltpu.SemaphoreType.DMA((STEPS,)),
             pltpu.SemaphoreType.DMA((STEPS,)),
             pltpu.SemaphoreType.DMA((STEPS,)),
             pltpu.SemaphoreType.DMA((STEPS + 1,)),

time: 24.5 us -> 24.5 us (level)
  no operation moved by 1% of the time
where the time goes in v7:
time: 24.5 us; the launch traced here: 24.4 us
  Pallas kernels  23.7 us (97%)
  between operations  0.64 us (3%)
    pallas_call x1, Pallas kernels, on_device(): pl.pallas_call(kernel, out_shape=(jax.ShapeDtypeStruct(states.shape, F32)...  22.4 us
    pallas_call x1, Pallas kernels, on_device(): pl.pallas_call(write_out, out_shape=tuple((jax.ShapeDtypeStruct(array.sha...  1.37 us

profile of v7, /device:TPU:1, one launch (start us, length us, event | category | flops | bytes accessed | tf_op | source)
XLA Modules:
  0.0 24.4 jit_solution(14401145190712822824)
XLA Ops:
  0.6 22.4 %shard_map.148 = (f32[57,64,128]{2,1,0:T(8,128)S(1)}, f32[64,128]{1,0:T(8,128)S(1)}, f32[2,32,8,128]{3,2,1,0:T(8,128)S(1)}) custom-call(f32[57,64,128]{2,1,0:T(8,128)} %states_hbm.1, f32[64,128]{1,0:T(8,128)} %volt_hbm.1, f32[57,57]{1,0:T(8,128)} %coup_hbm.1, f32[1,57]{1,0:T(1,128)} %bitcast.7, f32[1,57]{1,0:T(1,128)} %bitcast.8, f32[1,57]{1,0:T(1,128)} %bitcast.9, ...), custom_call_target="tpu_custom_call" | custom-call | tf_op jit(solution)/shard_map/pallas_call | solution.py:655
  23.0 1.4 %shard_map.149 = (f32[57,64,128]{2,1,0:T(8,128)}, f32[64,128]{1,0:T(8,128)}, f32[2,32,8,128]{3,2,1,0:T(8,128)}) custom-call(f32[57,64,128]{2,1,0:T(8,128)S(1)} %get-tuple-element.6.states, f32[64,128]{1,0:T(8,128)S(1)} %get-tuple-element.7.voltage, f32[2,32,8,128]{3,2,1,0:T(8,128)S(1)} %get-tuple-element.8.potential), custom_call_target="tpu_custom_call" | custom-call | tf_op jit(solution)/shard_map/pallas_call | solution.py:726
